TPU v7x, 512 devices: a whole 4x8x8 slice. The times are simulated.
512 devices in a mesh: dp: 16 (over y, core), ctx: 32 (over z, x).
Axes of the slice: x: 4, y: 8, z: 8, core: 2. Of those that a mesh axis runs over, the one named last changes fastest.
Arguments:
- queries: bfloat16 [16, 4096, 4096], P('dp', 'ctx'), may hold values from -9 to 9
- keys: bfloat16 [16, 4096, 1024], P('dp', 'ctx'), may hold values from -9 to 9
- values: bfloat16 [16, 4096, 1024], P('dp', 'ctx'), may hold values from -6 to 6
- doc_lengths: int32 [16, 128], P('dp'), may hold values from 1 to 128, as said below
- cotangent: float32 [16, 128, 4096], P('dp', 'ctx'), may hold values from -50 to 50
- query_gain: float32 [128], replicated, may hold values from 0.6 to 4.5
- key_gain: float32 [128], replicated, may hold values from 0.6 to 4.5
Outputs:
- embed_quarter: float32 [16, 128, 1024], P('dp', 'ctx')
- embed_half: float32 [16, 128, 2048], P('dp', 'ctx')
- embed_full: float32 [16, 128, 4096], P('dp', 'ctx')
- grad_queries: bfloat16 [16, 4096, 4096], P('dp', 'ctx')
- grad_keys: bfloat16 [16, 4096, 1024], P('dp', 'ctx')
- grad_values: bfloat16 [16, 4096, 1024], P('dp', 'ctx')
- grad_query_gain: float32 [128], replicated
- grad_key_gain: float32 [128], replicated
Inputs may be any that keep to these rules, and one draw needn't show every extreme that they name: `doc_lengths`: each sequence's 128 lengths sum to 4096; the first of them is exactly 128. The last 65 documents of each sequence together span at most 128 tokens.
All inputs are finite; a program needn't handle non-finite values.
Results may differ from a plain program's by a relative error of at most 0.0054.
The roundings to bfloat16 on the way count: a program that leaves them out, or rounds other values in their place, can miss the bound.
Values may be sent and summed in bfloat16 or wider, within the bound.
A program may use at most 64 MiB of HBM per device.

v0:
```python
import math

import jax
import jax.numpy as jnp
from jax import lax
from jax.sharding import PartitionSpec as P

EPS = 1e-06


def rms_forward(field, gain):
    inverse = lax.rsqrt(jnp.mean(field * field, axis=-1, keepdims=True) + EPS)
    unit = field * inverse
    return (unit * gain, unit, inverse)


def rms_backward(grad, unit, inverse, gain):
    scaled = grad * gain
    inner = jnp.mean(scaled * unit, axis=-1, keepdims=True)
    grad_in = inverse * (scaled - unit * inner)
    grad_gain = jnp.sum((grad * unit).reshape(-1, unit.shape[-1]), axis=0)
    return (grad_in, grad_gain)


def doc_ids(lengths, positions, total):
    ends = jnp.cumsum(lengths, dtype=jnp.int32)
    owner = jnp.sum((positions[:, None] >= ends[None, :]).astype(jnp.int32), axis=1)
    inside = (positions >= 0) & (positions < total)
    return jnp.where(inside, owner, -1)


def block_probs(queries, keys, query_ids, key_ids):
    rows, heads, width = queries.shape
    query_groups = keys.shape[1]
    grouped = queries.reshape(rows, query_groups, heads // query_groups, width)
    scores = jnp.einsum("rgpe,kge->gprk", grouped, keys, preferred_element_type=jnp.float32) * (
        1.0 / math.sqrt(width)
    )
    allowed = query_ids[:, None] == key_ids[None, :]
    scores = jnp.where(allowed[None, None], scores, -jnp.inf)
    top = jnp.max(scores, axis=-1, keepdims=True)
    powers = jnp.exp(scores - top)
    return (powers / jnp.sum(powers, axis=-1, keepdims=True), grouped)


def forward_block(queries, keys, values, query_ids, key_ids):
    probs, grouped = block_probs(queries, keys, query_ids, key_ids)
    low = probs.astype(jnp.bfloat16)
    mixed = jnp.einsum("gprk,kge->rgpe", low, values, preferred_element_type=jnp.float32)
    return mixed.reshape(queries.shape[0], -1).astype(jnp.bfloat16)


def backward_block(queries, keys, values, query_ids, key_ids, grad_out):
    probs, grouped = block_probs(queries, keys, query_ids, key_ids)
    low = probs.astype(jnp.bfloat16)
    rows, heads, width = queries.shape
    query_groups = keys.shape[1]
    grad_four = grad_out.reshape(rows, query_groups, heads // query_groups, width)
    grad_probs = jnp.einsum("rgpe,kge->gprk", grad_four, values, preferred_element_type=jnp.float32)
    inner = jnp.sum(probs * grad_probs, axis=-1, keepdims=True)
    grad_scores = (probs * (grad_probs - inner)).astype(jnp.bfloat16)
    scale = 1.0 / math.sqrt(width)
    grad_q = (
        jnp.einsum("gprk,kge->rgpe", grad_scores, keys, preferred_element_type=jnp.float32) * scale
    )
    grad_k = (
        jnp.einsum("gprk,rgpe->kge", grad_scores, grouped, preferred_element_type=jnp.float32)
        * scale
    )
    grad_v = jnp.einsum("gprk,rgpe->kge", low, grad_four, preferred_element_type=jnp.float32)
    return (grad_q.reshape(rows, heads, width), grad_k, grad_v)


def band_setup(keys, values, lengths, margin, total):
    key_pad = jnp.pad(keys, ((margin, margin), (0, 0), (0, 0)))
    value_pad = jnp.pad(values, ((margin, margin), (0, 0), (0, 0)))
    pad_ids = doc_ids(lengths, jnp.arange(total + 2 * margin, dtype=jnp.int32) - margin, total)
    return (key_pad, value_pad, pad_ids)


def band_forward(normed, padded, token_ids, margin):
    key_pad, value_pad, pad_ids = padded
    total = normed.shape[0]
    block = min(512, 4 * margin)
    window = block + 2 * margin

    def forward(index):
        start = index * block
        return forward_block(
            lax.dynamic_slice_in_dim(normed, start, block, 0),
            lax.dynamic_slice_in_dim(key_pad, start, window, 0),
            lax.dynamic_slice_in_dim(value_pad, start, window, 0),
            lax.dynamic_slice_in_dim(token_ids, start, block, 0),
            lax.dynamic_slice_in_dim(pad_ids, start, window, 0),
        )

    return lax.map(forward, jnp.arange(total // block, dtype=jnp.int32)).reshape(total, -1)


def band_backward(normed, padded, token_ids, margin, grad_out):
    key_pad, value_pad, pad_ids = padded
    total, heads, width = normed.shape
    block = min(512, 4 * margin)
    window = block + 2 * margin
    zeros = jnp.zeros(key_pad.shape, jnp.float32)

    def backward(carry, index):
        key_acc, value_acc = carry
        start = index * block
        grad_q, grad_k, grad_v = backward_block(
            lax.dynamic_slice_in_dim(normed, start, block, 0),
            lax.dynamic_slice_in_dim(key_pad, start, window, 0),
            lax.dynamic_slice_in_dim(value_pad, start, window, 0),
            lax.dynamic_slice_in_dim(token_ids, start, block, 0),
            lax.dynamic_slice_in_dim(pad_ids, start, window, 0),
            lax.dynamic_slice_in_dim(grad_out, start, block, 0),
        )
        key_acc = lax.dynamic_update_slice_in_dim(
            key_acc, lax.dynamic_slice_in_dim(key_acc, start, window, 0) + grad_k, start, 0
        )
        value_acc = lax.dynamic_update_slice_in_dim(
            value_acc, lax.dynamic_slice_in_dim(value_acc, start, window, 0) + grad_v, start, 0
        )
        return ((key_acc, value_acc), grad_q)

    (key_acc, value_acc), grad_blocks = lax.scan(
        backward, (zeros, zeros), jnp.arange(total // block, dtype=jnp.int32)
    )
    return (
        grad_blocks.reshape(total, heads, width),
        key_acc[margin : margin + total],
        value_acc[margin : margin + total],
    )


def matryoshka(pooled, cotangent):
    width = pooled.shape[-1]
    prefixes = (width // 4, width // 2, width)

    def embed(field):
        return tuple(
            (
                field[:, :count]
                * lax.rsqrt(
                    jnp.sum(field[:, :count] * field[:, :count], axis=-1, keepdims=True) + EPS
                )
                for count in prefixes
            )
        )

    embeds, pullback = jax.vjp(embed, pooled)
    (grad,) = pullback(tuple((cotangent[:, :count] for count in prefixes)))
    return (embeds, grad)


def pool_tokens(attended, token_ids, docs, own_lengths):
    onehot = (token_ids[:, None] == jnp.arange(docs, dtype=jnp.int32)[None, :]).astype(jnp.bfloat16)
    partial_sums = jnp.dot(onehot.T, attended, preferred_element_type=jnp.float32)
    return lax.psum_scatter(partial_sums, "ctx", scatter_dimension=0, tiled=True) / own_lengths


def spread_tokens(scaled, token_ids):
    whole = lax.all_gather(scaled.astype(jnp.bfloat16), "ctx", axis=0, tiled=True).astype(
        scaled.dtype
    )
    return jnp.take(whole, token_ids, axis=0).astype(jnp.bfloat16)


def body(queries, keys, values, doc_lengths, cotangent, query_gain, key_gain):
    rows = queries.shape[1]
    model = queries.shape[2]
    width = query_gain.shape[0]
    heads = model // width
    kv_width = keys.shape[2]
    query_groups = kv_width // width
    group_repeat = heads // query_groups
    shards = lax.axis_size("ctx")
    position = lax.axis_index("ctx")
    total = rows * shards
    lengths = doc_lengths[0]
    docs = lengths.shape[0]
    owned = docs // shards
    own_ids = doc_ids(lengths, position * rows + jnp.arange(rows, dtype=jnp.int32), total)
    own_lengths = lax.dynamic_slice_in_dim(lengths, position * owned, owned).astype(jnp.float32)[
        :, None
    ]
    normed_kf, unit_k, inv_k = rms_forward(
        keys[0].astype(jnp.float32).reshape(rows, query_groups, width), key_gain
    )
    normed_k = normed_kf.astype(jnp.bfloat16)
    key_rep = jnp.repeat(normed_k, group_repeat, axis=1).reshape(rows, model)
    value_rep = jnp.repeat(
        values[0].reshape(rows, query_groups, width), group_repeat, axis=1
    ).reshape(rows, model)
    head_q, head_k, head_v = (
        lax.all_to_all(queries[0], "ctx", split_axis=1, concat_axis=0, tiled=True),
        lax.all_to_all(key_rep, "ctx", split_axis=1, concat_axis=0, tiled=True),
        lax.all_to_all(value_rep, "ctx", split_axis=1, concat_axis=0, tiled=True),
    )
    local_heads = model // shards // width
    normed_qf, unit_q, inv_q = rms_forward(
        head_q.astype(jnp.float32).reshape(total, local_heads, width), query_gain
    )
    normed_q = normed_qf.astype(jnp.bfloat16)
    all_ids = doc_ids(lengths, jnp.arange(total, dtype=jnp.int32), total)
    padded = band_setup(
        head_k.reshape(total, local_heads, width),
        head_v.reshape(total, local_heads, width),
        lengths,
        rows,
        total,
    )
    attended = band_forward(normed_q, padded, all_ids, rows)
    back_rows = lax.all_to_all(attended, "ctx", split_axis=0, concat_axis=1, tiled=True)
    pooled = pool_tokens(back_rows, own_ids, docs, own_lengths)
    embeds, grad_pooled = matryoshka(pooled, cotangent[0])
    grad_rows = spread_tokens(grad_pooled / own_lengths, own_ids)
    grad_out = lax.all_to_all(grad_rows, "ctx", split_axis=1, concat_axis=0, tiled=True)
    grad_nq, grad_head_k, grad_head_v = band_backward(normed_q, padded, all_ids, rows, grad_out)
    grad_qf, grad_qgain = rms_backward(grad_nq, unit_q, inv_q, query_gain)
    grad_q = lax.all_to_all(
        grad_qf.astype(jnp.bfloat16).reshape(total, local_heads * width),
        "ctx",
        split_axis=0,
        concat_axis=1,
        tiled=True,
    )
    share_k, share_v = (
        lax.all_to_all(
            grad_head_k.reshape(total, local_heads * width),
            "ctx",
            split_axis=0,
            concat_axis=1,
            tiled=True,
        ),
        lax.all_to_all(
            grad_head_v.reshape(total, local_heads * width),
            "ctx",
            split_axis=0,
            concat_axis=1,
            tiled=True,
        ),
    )
    grad_nk = jnp.sum(share_k.reshape(rows, query_groups, group_repeat, width), axis=2)
    grad_vf = jnp.sum(share_v.reshape(rows, query_groups, group_repeat, width), axis=2)
    grad_kf, grad_kgain = rms_backward(grad_nk, unit_k, inv_k, key_gain)
    total_qgain, total_kgain = lax.psum((grad_qgain, grad_kgain), ("dp", "ctx"))
    return (
        embeds[0][None],
        embeds[1][None],
        embeds[2][None],
        grad_q[None],
        grad_kf.astype(jnp.bfloat16).reshape(rows, kv_width)[None],
        grad_vf.astype(jnp.bfloat16).reshape(rows, kv_width)[None],
        total_qgain,
        total_kgain,
    )


def solution(mesh):
    in_specs = (
        P("dp", "ctx", None),
        P("dp", "ctx", None),
        P("dp", "ctx", None),
        P("dp", None),
        P("dp", "ctx", None),
        P(),
        P(),
    )
    out_specs = (
        P("dp", "ctx", None),
        P("dp", "ctx", None),
        P("dp", "ctx", None),
        P("dp", "ctx", None),
        P("dp", "ctx", None),
        P("dp", "ctx", None),
        P(),
        P(),
    )
    return jax.shard_map(body, mesh=mesh, in_specs=in_specs, out_specs=out_specs, check_vma=False)
```

profile of v0, /device:TPU:1, one launch (start us, length us, event | category | flops | bytes accessed | tf_op | source)
XLA Modules:
  0.0 838.3 jit_solution(9058164657707362389)
XLA Ops:
  9.4 13.7 %all-to-all-start = ((bf16[128,32,128]{2,0,1:T(8,128)(2,1)}), bf16[128,32,128]{2,0,1:T(8,128)(2,1)S(1)}, u32[]{:S(2)}, u32[]{:S(2)}) async-start(bf16[128,32,128]{2,0,1:T(8,128)(2,1)} %bitcast.29), calls=%async_computation | async-start | bytes 2097152 | tf_op jit(solution)/shard_map/all_to_all | solution.py:198
  24.8 24.6 %all-to-all-done = bf16[128,32,128]{2,0,1:T(8,128)(2,1)S(1)} async-done(((bf16[128,32,128]{2,0,1:T(8,128)(2,1)}), bf16[128,32,128]{2,0,1:T(8,128)(2,1)S(1)}, u32[]{:S(2)}, u32[]{:S(2)}) %all-to-all-start) | async-done | bytes 1048608 | tf_op jit(solution)/shard_map/all_to_all | solution.py:198
  50.6 6.4 all-to-all-start.1
  57.0 2.3 copy.106
  59.3 23.0 %all-to-all-done.1 = bf16[128,32,128]{2,0,1:T(8,128)(2,1)S(1)} async-done(((bf16[128,32,128]{2,0,1:T(8,128)(2,1)}), bf16[128,32,128]{2,0,1:T(8,128)(2,1)S(1)}, u32[]{:S(2)}, u32[]{:S(2)}) %all-to-all-start.1) | async-done | bytes 1048608 | tf_op jit(solution)/shard_map/all_to_all | solution.py:197
  82.2 6.8 all-to-all-start.2
  90.1 2.6 convert_reduce_fusion
  95.0 18.5 %all-to-all-done.2 = bf16[128,32,128]{0,2,1:T(8,128)(2,1)S(1)} async-done(((bf16[128,32,128]{0,2,1:T(8,128)(2,1)}), bf16[128,32,128]{0,2,1:T(8,128)(2,1)S(1)}, u32[]{:S(2)}, u32[]{:S(2)}) %all-to-all-start.2) | async-done | bytes 1048608 | tf_op jit(solution)/shard_map/all_to_all | solution.py:196
  113.5 1.7 convert_bitcast_fusion
  115.1 1.9 copy.107
  117.4 1.7 fusion.44
  119.0 41.8 %while.24 = (s32[]{:T(128)}, bf16[8,512,128]{2,1,0:T(8,128)(2,1)}, s32[8]{0:T(128)S(1)}, bf16[4352,1,128]{2,0,1:T(8,128)(2,1)}, s32[4096]{0:T(1024)S(1)}, /*inde...) while((s32[]{:T(128)}, bf16[8,512,128]{2,1,0:T(8,128)(2,1)}, ...), condition=%wide.region_9.10_spmd, body=%wide.region_6.9_spmd.sunk | while | flops 204930048 | bytes 5924080 | solution.py:97
  120.4 1.4 fusion.88
  125.7 1.4 fusion.88
  130.9 1.4 fusion.88
  132.6 1.4 fusion.90
  136.1 1.4 fusion.88
  141.3 1.4 fusion.88
  143.0 1.4 fusion.90
  146.6 1.4 fusion.88
  151.8 1.4 fusion.88
  157.0 1.4 fusion.88
  160.9 7.4 all-to-all-start.3
  168.5 24.6 %all-to-all-done.3 = bf16[32,128,128]{2,1,0:T(8,128)(2,1)S(1)} async-done(((bf16[32,128,128]{2,1,0:T(8,128)(2,1)}), bf16[32,128,128]{2,1,0:T(8,128)(2,1)S(1)}, u32[]{:S(2)}, u32[]{:S(2)}) %all-to-all-start.3) | async-done | bytes 1048608 | tf_op jit(solution)/shard_map/all_to_all | solution.py:214
  193.8 1.8 fusion.55
  197.7 160.3 %all-reduce.10.cloned.1.call-done = f32[128,4096]{1,0:T(8,128)} async-done(((f32[128,4096]{1,0:T(8,128)}), f32[128,4096]{1,0:T(8,128)}) %all-reduce.10.cloned.1.call-update) | async-done | bytes 2097168
  361.7 79.2 %all-gather.3.cloned.1.call-done = bf16[32,4,4096]{2,1,0:T(4,128)(2,1)} async-done(((bf16[1,4,4096]{2,1,0:T(4,128)(2,1)}), bf16[32,4,4096]{2,1,0:T(4,128)(2,1)}) %all-gather.3.cloned.1.call-update) | async-done | bytes 1048592 | tf_op jit(solution)/shard_map/all_gather | solution.py:163
  444.8 5.9 all-to-all-start.4
  451.4 21.0 %all-to-all-done.4 = bf16[128,32,128]{2,0,1:T(8,128)(2,1)} async-done(((bf16[128,32,128]{2,0,1:T(8,128)(2,1)}), bf16[128,32,128]{2,0,1:T(8,128)(2,1)}, u32[]{:S(2)}, u32[]{:S(2)}) %all-to-all-start.4) | async-done | bytes 1048608 | tf_op jit(solution)/shard_map/all_to_all | solution.py:218
  472.4 1.5 broadcast_in_dim.113.clone
  473.9 1.5 broadcast_in_dim.113.clone2
  475.4 106.8 %while.25 = (s32[]{:T(128)}, f32[4352,1,128]{2,0,1:T(8,128)}, f32[4352,1,128]{2,0,1:T(8,128)}, f32[8,512,1,128]{3,1,0,2:T(8,128)}, s32[8]{0:T(128)S(1)}, /*index...) while((s32[]{:T(128)}, f32[4352,1,128]{2,0,1:T(8,128)}, ...), condition=%wide.region_21.22_spmd, body=%wide.region_17.21_spmd.sunk | while | flops 510753280 | bytes 23696676 | solution.py:126
  478.0 1.4 fusion.97
  482.4 1.4 fusion.100
  491.4 1.4 fusion.97
  495.8 1.4 fusion.100
  504.7 1.4 fusion.97
  509.1 1.4 fusion.100
  518.1 1.4 fusion.97
  522.5 1.4 fusion.100
  531.4 1.4 fusion.97
  535.8 1.4 fusion.100
  544.8 1.4 fusion.97
  549.1 1.4 fusion.100
  558.1 1.4 fusion.97
  562.5 1.4 fusion.100
  571.5 1.4 fusion.97
  575.8 1.4 fusion.100
  582.2 3.1 copy.112
  585.3 3.1 multiply_reduce_fusion
  589.0 3.3 multiply_convert_fusion
  592.3 7.0 all-to-all-start.5
  599.4 1.5 slice.26
  600.8 2.9 copy.117
  603.8 17.2 %all-to-all-done.5 = bf16[32,128,128]{1,2,0:T(8,128)(2,1)S(1)} async-done(((bf16[32,128,128]{1,2,0:T(8,128)(2,1)}), bf16[32,128,128]{1,2,0:T(8,128)(2,1)S(1)}, u32[]{:S(2)}, u32[]{:S(2)}) %all-to-all-start.5) | async-done | bytes 1048608 | tf_op jit(solution)/shard_map/all_to_all | solution.py:221
  622.0 7.2 all-to-all-start.6
  629.2 3.1 slice.27
  632.3 2.9 copy.121
  635.2 38.2 %all-to-all-done.6 = f32[32,128,128]{1,2,0:T(8,128)S(1)} async-done(((f32[32,128,128]{1,2,0:T(8,128)}), f32[32,128,128]{1,2,0:T(8,128)S(1)}, u32[]{:S(2)}, u32[]{:S(2)}) %all-to-all-start.6) | async-done | bytes 2097184 | tf_op jit(solution)/shard_map/all_to_all | solution.py:229
  673.4 8.6 %all-to-all-start.7 = ((f32[32,128,128]{1,2,0:T(8,128)}), f32[32,128,128]{1,2,0:T(8,128)}, u32[]{:S(2)}, u32[]{:S(2)}) async-start(f32[32,128,128]{1,2,0:T(8,128)} %copy.121), calls=%async_computation.7 | async-start | bytes 4194304 | tf_op jit(solution)/shard_map/all_to_all | solution.py:236
  682.0 2.3 copy.125
  686.2 40.4 %all-to-all-done.7 = f32[32,128,128]{1,2,0:T(8,128)} async-done(((f32[32,128,128]{1,2,0:T(8,128)}), f32[32,128,128]{1,2,0:T(8,128)}, u32[]{:S(2)}, u32[]{:S(2)}) %all-to-all-start.7) | async-done | bytes 2097184 | tf_op jit(solution)/shard_map/all_to_all | solution.py:236
  726.6 1.8 bitcast_reduce_fusion
  729.5 102.0 %all-reduce.7 = (f32[128]{0:T(128)}, f32[128]{0:T(128)}) all-reduce(f32[128]{0:T(128)S(1)} %copy-done.19, f32[128]{0:T(128)S(1)} %bitcast_reduce_fusion.2), channel_id=1, replica_groups=mesh['dp'=16,'ctx'=32] {'dp','ctx'}, use_global_device_ids=true, to_apply=%region_27.28 | all-reduce | flops 256 | bytes 2048 | tf_op jit(solution)/shard_map/psum | solution.py:247
  (291 shorter events, 124.5 us)
Async XLA Ops:
  8.2 15.0 %copy-start.9 = (bf16[1,128,1024]{2,1,0:T(8,128)(2,1)S(1)}, bf16[1,128,1024]{2,1,0:T(8,128)(2,1)}, u32[]{:S(2)}) copy-start(bf16[1,128,1024]{2,1,0:T(8,128)(2,1)} %param.12) | copy-start | bytes 786436
  8.2 16.0 %copy-start.13 = (f32[128]{0:T(128)S(1)}, f32[128]{0:T(128)}, u32[]{:S(2)}) copy-start(f32[128]{0:T(128)} %param.17) | copy-start | bytes 1540
  9.4 39.9 %all-to-all-start = ((bf16[128,32,128]{2,0,1:T(8,128)(2,1)}), bf16[128,32,128]{2,0,1:T(8,128)(2,1)S(1)}, u32[]{:S(2)}, u32[]{:S(2)}) async-start(bf16[128,32,128]{2,0,1:T(8,128)(2,1)} %bitcast.29), calls=%async_computation | async-start | bytes 2097152 | tf_op jit(solution)/shard_map/all_to_all | solution.py:198
  23.4 0.8 copy-start.5
  23.4 27.1 %copy-start.10 = (f32[128,8]{0,1:T(8,128)}, f32[128,8]{0,1:T(8,128)S(1)}, u32[]{:S(2)}) copy-start(f32[128,8]{0,1:T(8,128)S(1)} %add_rsqrt_fusion.1) | copy-start | bytes 12292
  50.6 31.6 %all-to-all-start.1 = ((bf16[128,32,128]{2,0,1:T(8,128)(2,1)}), bf16[128,32,128]{2,0,1:T(8,128)(2,1)S(1)}, u32[]{:S(2)}, u32[]{:S(2)}) async-start(bf16[128,32,128]{2,0,1:T(8,128)(2,1)} %bitcast.33), calls=%async_computation.1 | async-start | bytes 2097152 | tf_op jit(solution)/shard_map/all_to_all | solution.py:197
  57.0 32.1 %copy-start.17 = (s32[1,128]{1,0:T(1,128)S(1)}, s32[1,128]{1,0:T(1,128)}, u32[]{:S(2)}) copy-start(s32[1,128]{1,0:T(1,128)} %param.14) | copy-start | bytes 1540
  82.2 31.2 %all-to-all-start.2 = ((bf16[128,32,128]{0,2,1:T(8,128)(2,1)}), bf16[128,32,128]{0,2,1:T(8,128)(2,1)S(1)}, u32[]{:S(2)}, u32[]{:S(2)}) async-start(bf16[128,32,128]{0,2,1:T(8,128)(2,1)} %bitcast.243), calls=%async_computation.2 | async-start | bytes 2097152 | tf_op jit(solution)/shard_map/all_to_all | solution.py:196
  113.5 3.6 copy-start.3
  115.1 2.2 copy-start.15
  117.1 2.0 copy-start
  160.9 32.3 %all-to-all-start.3 = ((bf16[32,128,128]{2,1,0:T(8,128)(2,1)}), bf16[32,128,128]{2,1,0:T(8,128)(2,1)S(1)}, u32[]{:S(2)}, u32[]{:S(2)}) async-start(bf16[32,128,128]{2,1,0:T(8,128)(2,1)} %bitcast.247), calls=%async_computation.3 | async-start | bytes 2097152 | tf_op jit(solution)/shard_map/all_to_all | solution.py:214
  168.3 189.7 %all-reduce.10.cloned.1.call-start = ((), (), s32[]{:S(2)}) async-start(), calls=%async_computation.9 | async-start | bytes 4194304
  193.8 3.9 copy-start.18
  193.8 164.2 %copy-start.8 = (f32[1,4,4096]{2,1,0:T(4,128)S(1)}, f32[1,4,4096]{2,1,0:T(4,128)}, u32[]{:S(2)}) copy-start(f32[1,4,4096]{2,1,0:T(4,128)} %param.15) | copy-start | bytes 196612
  195.6 245.3 %all-gather.3.cloned.1.call-start = ((), (), s32[]{:S(2)}) async-start(), calls=%async_computation.8 | async-start | bytes 1081344 | tf_op jit(solution)/shard_map/all_gather | solution.py:163
  444.8 27.6 %all-to-all-start.4 = ((bf16[128,32,128]{2,0,1:T(8,128)(2,1)}), bf16[128,32,128]{2,0,1:T(8,128)(2,1)}, u32[]{:S(2)}, u32[]{:S(2)}) async-start(bf16[128,32,128]{2,0,1:T(8,128)(2,1)} %fusion.42), calls=%async_computation.4 | async-start | bytes 2097152 | tf_op jit(solution)/shard_map/all_to_all | solution.py:218
  582.2 3.1 copy-start.1
  582.2 3.1 copy-start.12
  582.2 3.1 copy-start.16
  585.3 3.8 copy-start.4
  589.0 10.3 %copy-start.2 = (f32[4352,1,128]{2,0,1:T(8,128)S(1)}, f32[4352,1,128]{2,0,1:T(8,128)}, u32[]{:S(2)}) copy-start(f32[4352,1,128]{2,0,1:T(8,128)} %get-tuple-element.111) | copy-start | bytes 6684676
  592.3 28.6 %all-to-all-start.5 = ((bf16[32,128,128]{1,2,0:T(8,128)(2,1)}), bf16[32,128,128]{1,2,0:T(8,128)(2,1)S(1)}, u32[]{:S(2)}, u32[]{:S(2)}) async-start(bf16[32,128,128]{1,2,0:T(8,128)(2,1)} %multiply_convert_fusion), calls=%async_computation.5 | async-start | bytes 2097152 | tf_op jit(solution)/shard_map/all_to_all | solution.py:221
  621.0 1.0 copy-start.7
  622.0 51.4 %all-to-all-start.6 = ((f32[32,128,128]{1,2,0:T(8,128)}), f32[32,128,128]{1,2,0:T(8,128)S(1)}, u32[]{:S(2)}, u32[]{:S(2)}) async-start(f32[32,128,128]{1,2,0:T(8,128)} %copy.117), calls=%async_computation.6 | async-start | bytes 4194304 | tf_op jit(solution)/shard_map/all_to_all | solution.py:229
  635.1 46.8 %copy-start.14 = (f32[128]{0:T(128)S(1)}, f32[128]{0:T(128)}, u32[]{:S(2)}) copy-start(f32[128]{0:T(128)} %param.17) | copy-start | bytes 1540
  673.4 53.3 %all-to-all-start.7 = ((f32[32,128,128]{1,2,0:T(8,128)}), f32[32,128,128]{1,2,0:T(8,128)}, u32[]{:S(2)}, u32[]{:S(2)}) async-start(f32[32,128,128]{1,2,0:T(8,128)} %copy.121), calls=%async_computation.7 | async-start | bytes 4194304 | tf_op jit(solution)/shard_map/all_to_all | solution.py:236
  681.9 2.5 copy-start.6
  682.0 2.5 copy-start.11
  686.2 43.3 %copy-start.19 = (f32[128]{0:T(128)S(1)}, f32[128]{0:T(128)}, u32[]{:S(2)}) copy-start(f32[128]{0:T(128)} %get-tuple-element.153) | copy-start | bytes 1540
Sparse Core Ops, SparseCore 0:
  195.8 162.1 all-reduce.9
  362.2 78.6 all-gather.2
where the time goes:
time: 841 us; the launch traced here: 838 us
  waiting for transfers between devices  447 us (53%)
  blocking collectives  102 us (12%)
  local copies, waits for them, and re-layouts  92.7 us (11%)
  matrix products  77.2 us (9%)
  starting transfers between devices  63.1 us (8%)
  other arithmetic  29.8 us (4%)
  between operations  15.2 us (2%)
  loops' own time  11.5 us (1%)
    unnamed x3, waiting for transfers between devices  160 us
    psum x1, blocking collectives, body(): total_qgain, total_kgain = lax.psum((grad_qgain, grad_kgain), ('dp', 'ctx'))  102 us
    all_gather x1, waiting for transfers between devices, spread_tokens(): lax.all_gather(scaled.astype(jnp.bfloat16), 'ctx', axis=0, tiled=True)  79.2 us
    all_to_all x1, waiting for transfers between devices, body(): lax.all_to_all(grad_head_v.reshape(total, local_heads * width), 'ctx', sp...  40.4 us
    all_to_all x1, waiting for transfers between devices, body(): lax.all_to_all(grad_head_k.reshape(total, local_heads * width), 'ctx', sp...  38.2 us
    all_to_all x1, waiting for transfers between devices, body(): lax.all_to_all(value_rep, 'ctx', split_axis=1, concat_axis=0, tiled=True)  24.6 us
    all_to_all x1, waiting for transfers between devices, body(): lax.all_to_all(attended, 'ctx', split_axis=0, concat_axis=1, tiled=True)  24.6 us
    all_to_all x1, waiting for transfers between devices, body(): lax.all_to_all(key_rep, 'ctx', split_axis=1, concat_axis=0, tiled=True)  23 us
  transfers between devices with their start and end apart: 10, of which 10 were waited for; matrix products, arithmetic and copies ran while one was open for 3% of the time, Pallas kernels for 0%

commit v1 on v0

v1 whole, which is shorter than its diff:
```python
import functools
import math

import jax
import jax.numpy as jnp
from jax import lax
from jax.experimental import pallas as pl
from jax.experimental.pallas import tpu as pltpu
from jax.sharding import PartitionSpec as P

EPS = 1e-06
T = 128
G = 8
R = 4
W = 4096
NX, NZ = 4, 8
C = 1024
SCALE = 1.0 / math.sqrt(T)
LOG2E = 1.4426950408889634
NEG = -1e30
F32, BF16 = jnp.float32, jnp.bfloat16
MESH = pl.DeviceIdType.MESH
LAST = NX * NZ - 1
HALF = NX * NZ // 2
NT = (((1,), (1,)), ((), ()))
TN = (((0,), (0,)), ((), ()))


def iota(shape, dim):
    return lax.broadcasted_iota(jnp.int32, shape, dim)


def dot(a, b, dims=(((1,), (0,)), ((), ()))):
    return lax.dot_general(a, b, dims, preferred_element_type=F32)


def rows_of(start, size):
    return pl.ds(pl.multiple_of(start, 16), size)


def cols_of(start, size):
    return pl.ds(pl.multiple_of(start, 128), size)


def kernel(
    ny, nc,
    q_ref, k_ref, v_ref, len_ref, cot_ref, qg_ref, kg_ref,
    eq_ref, eh_ref, ef_ref, gq_ref, gk_ref, gv_ref, qgain_ref, kgain_ref,
    halo, kn, uk, ik, vw, qn, uq, iq, pr, bias, att, pool, tokc, ga, rows_s, rows_r,
    blk32, blk, cot_a, cot_b, s2, s2b, rx, zs, rz, rb, dss, lows, dos, dh_s, dh_r, dk_own, dv_own,
    gz, gy, gx,
    h_snd, h_rcv, r_snd, r_rcv, cz_snd, cz_rcv, cx_snd, cx_rcv, cb_snd, cb_rcv,
    px_snd, px_rcv, pz_snd, pz_rcv, pb_snd, pb_rcv, d_snd, d_rcv,
    gz_snd, gz_rcv, gy_snd, gy_rcv, gx_snd, gx_rcv,
):
    dp, ctx = lax.axis_index("dp"), lax.axis_index("ctx")
    z, x = ctx // NX, ctx % NX
    y, core = dp // nc, dp % nc
    nxt, prv = (ctx + 1) % (NX * NZ), (ctx + NX * NZ - 1) % (NX * NZ)
    low_half = z < NZ // 2
    sends_b = jnp.logical_and(ctx >= HALF, ctx < LAST)

    def at_z(i):
        return (dp, ((z + i) % NZ) * NX + x)

    def at_x(i):
        return (dp, z * NX + (x + i) % NX)

    def at_y(i):
        return (((y + i) % ny) * nc + core, ctx)

    barrier = pltpu.get_barrier_semaphore()

    def greet(device):
        pl.semaphore_signal(barrier, inc=1, device_id=device, device_id_type=MESH)

    for i in range(1, NZ):
        greet(at_z(i))
    for i in range(1, NX):
        greet(at_x(i))
    for i in range(1, ny):
        greet(at_y(i))
    for j in range(1, nc):
        for i in range(NX):
            greet((y * nc + (core + j) % nc, z * NX + (x + i) % NX))

    @pl.when(x == NX - 1)
    def _():
        greet((dp, nxt))

    @pl.when(x == 0)
    def _():
        greet((dp, prv))

    @pl.when(sends_b)
    def _():
        greet((dp, LAST))

    @pl.when(ctx == LAST)
    def _():
        @pl.loop(HALF, LAST)
        def _(c):
            greet((dp, c))

    count = (NZ - 1) + (NX - 1) + (ny - 1) + NX * (nc - 1)
    edge = jnp.where(jnp.logical_or(x == 0, x == NX - 1), 1, 0)
    far = jnp.where(ctx == LAST, LAST - HALF, jnp.where(sends_b, 1, 0))
    pl.semaphore_wait(barrier, count + edge + far)

    def remote(src, dst, snd, rcv, device):
        return pltpu.make_async_remote_copy(
            src_ref=src, dst_ref=dst, send_sem=snd, recv_sem=rcv, device_id=device, device_id_type=MESH
        )

    def halo_copy(g, i):
        src = (k_ref if i < 2 else v_ref).at[:, cols_of(g * T, T)]
        return remote(src, halo.at[g, i], h_snd.at[g, i], h_rcv.at[g, i], (dp, nxt if i % 2 == 0 else prv))

    @pl.loop(0, G)
    def _(g):
        for i in range(4):
            halo_copy(g, i).start()

    for c in range(4):
        blk32[c * 4 : c * 4 + 4, :] = cot_ref[:, c * C : (c + 1) * C]
    blk[...] = blk32[...].astype(BF16)

    def cz_copy(i):
        return remote(
            blk, cot_a.at[rows_of(x * 64 + z * 16, 16)], cz_snd.at[i], cz_rcv.at[z], at_z(i)
        )

    def cz_wait(zz):
        return remote(blk, cot_a.at[rows_of(x * 64 + zz * 16, 16)], cz_snd.at[0], cz_rcv.at[zz], at_z(1))

    def cx_copy(i):
        own = cot_a.at[rows_of(x * 64, 64)]
        return remote(own, own, cx_snd.at[i], cx_rcv.at[x], at_x(i))

    def cx_wait(i):
        own = cot_a.at[rows_of(((x + i) % NX) * 64, 64)]
        return remote(own, own, cx_snd.at[i], cx_rcv.at[(x + i) % NX], at_x(i))

    def cb_copy(c):
        return remote(
            blk, cot_b.at[rows_of((c - HALF) * 16, 16)], cb_snd.at[0], cb_rcv.at[c - HALF], (dp, LAST)
        )

    @pl.when(low_half)
    def _():
        cot_a[rows_of(x * 64 + z * 16, 16), :] = blk[...]
        for i in range(1, NZ):
            cz_copy(i).start()

    @pl.when(sends_b)
    def _():
        cb_copy(ctx).start()

    @pl.when(ctx == LAST)
    def _():
        cot_b[(HALF - 1) * 16 : HALF * 16, :] = blk[...]

    lens = jnp.broadcast_to(len_ref[...].astype(F32), (T, T))
    ii, jj = iota((T, T), 0), iota((T, T), 1)
    base = (ctx * T).astype(F32)

    def pick(cond, value, axis):
        return jnp.sum(jnp.where(cond, value, 0.0), axis=axis, keepdims=True)

    lens_col = pick(ii == jj, lens, 1)
    ends_col = pick(jj <= ii, lens, 1)
    ends_row = pick(ii <= jj, jnp.broadcast_to(lens_col, (T, T)), 0)
    starts = ends_row - lens[:1]
    ids_col = pick(base + ii.astype(F32) >= ends_row, 1.0, 1)
    key_pos = base - T + iota((T, 3 * T), 1).astype(F32)
    ids_row = jnp.where(key_pos[:1] < 0.0, -1.0, pick(key_pos >= ends_col, 1.0, 0))
    bias[...] = jnp.where(ids_col == ids_row, 0.0, NEG)
    own_row = ids_row[:, T : 2 * T]
    same = jnp.where(ids_col == own_row, 1.0, 0.0).astype(BF16)
    inv_len = 1.0 / pick(ids_col == jj.astype(F32), lens, 1)
    first_id = jnp.min(own_row, axis=1, keepdims=True)
    last_id = jnp.max(own_row, axis=1, keepdims=True)
    with_prv = jnp.where(ids_col == jnp.max(ids_row[:, :T], axis=1, keepdims=True), 1.0, 0.0)
    with_nxt = jnp.where(ids_col == jnp.min(ids_row[:, 2 * T :], axis=1, keepdims=True), 1.0, 0.0)
    r8 = iota((8, T), 0)
    ends8 = jnp.where(
        jnp.logical_or(
            jnp.logical_and(r8 == 0, own_row == first_id), jnp.logical_and(r8 == 1, own_row == last_id)
        ),
        1.0,
        0.0,
    ).astype(BF16)

    q_gain, k_gain = qg_ref[...], kg_ref[...]

    def forward(g):
        for i in range(4):
            halo_copy(g, i).wait_recv()
        cols = cols_of(g * T, T)
        for i, raw in enumerate((halo[g, 0], k_ref[:, cols], halo[g, 1])):
            raw = raw.astype(F32)
            inv = lax.rsqrt(jnp.mean(raw * raw, axis=-1, keepdims=True) + EPS)
            unit = raw * inv
            uk[g, i * T : (i + 1) * T, :] = unit
            kn[g, i * T : (i + 1) * T, :] = (unit * k_gain).astype(BF16)
            if i == 1:
                ik[g] = inv
        vw[g, :T, :] = halo[g, 2]
        vw[g, T : 2 * T, :] = v_ref[:, cols]
        vw[g, 2 * T :, :] = halo[g, 3]
        for p in range(R):
            cols = cols_of(g * (R * T) + p * T, T)
            rows = slice(p * T, (p + 1) * T)
            raw = q_ref[:, cols].astype(F32)
            inv = lax.rsqrt(jnp.mean(raw * raw, axis=-1, keepdims=True) + EPS)
            unit = raw * inv
            normed = (unit * q_gain).astype(BF16)
            uq[g, rows, :] = unit
            iq[g, rows, :] = inv
            qn[g, rows, :] = normed
            s = dot(normed, kn[g], NT) * (SCALE * LOG2E) + bias[...]
            powers = jnp.exp2(s - jnp.max(s, axis=-1, keepdims=True))
            probs = powers * (1.0 / jnp.sum(powers, axis=-1, keepdims=True))
            pr[g, rows, :] = probs
            att[:, cols] = dot(probs.astype(BF16), vw[g]).astype(BF16)

    @pl.loop(0, G // 2)
    def _(g):
        forward(g)

    for zz in range(NZ // 2):
        @pl.when(z != zz)
        def _():
            cz_wait(zz).wait_recv()
    for i in range(1, NX):
        cx_copy(i).start()

    @pl.loop(G // 2, G)
    def _(g):
        forward(g)

    for c in range(8):
        cols = slice(c * 512, (c + 1) * 512)
        ends = dot(ends8, att[:, cols])
        rows_s[0, :, cols] = ends[0:1]
        rows_s[1, :, cols] = ends[1:2]

    def row_copy(i):
        return remote(rows_s.at[i], rows_r.at[1 - i], r_snd.at[i], r_rcv.at[1 - i], (dp, prv if i == 0 else nxt))

    row_copy(0).start()
    row_copy(1).start()
    for c in range(8):
        cols = slice(c * 512, (c + 1) * 512)
        pool[:, cols] = dot(same, att[:, cols])

    for i in range(1, NX):
        cx_wait(i).wait_recv()
    rr = iota((1, 256), 1)
    doc_a = (((rr >> 4) & 3) * 16 + (rr >> 6) * 4 + (rr & 3)).astype(F32)
    doc_b = (64 + (rr >> 4) * 4 + (rr & 3)).astype(F32)
    quarter = (rr >> 2) & 3
    for c in range(8):
        cols = slice((c % 2) * 512, (c % 2 + 1) * 512)
        hot = jnp.where(jnp.logical_and(ids_col == doc_a, quarter == c // 2), 1.0, 0.0).astype(BF16)
        tokc[:, c * 512 : (c + 1) * 512] = dot(hot, cot_a[:, cols])

    @pl.when(ctx == LAST)
    def _():
        @pl.loop(HALF, LAST)
        def _(c):
            cb_copy(c).wait_recv()
        for c in range(8):
            cols = slice((c % 2) * 512, (c % 2 + 1) * 512)
            hot = jnp.where(jnp.logical_and(ids_col == doc_b, quarter == c // 2), 1.0, 0.0).astype(BF16)
            tokc[:, c * 512 : (c + 1) * 512] += dot(hot, cot_b[:, cols])

    row_copy(0).wait_recv()
    row_copy(1).wait_recv()
    norms, inners = [], []
    for c in range(8):
        cols = slice(c * 512, (c + 1) * 512)
        p = (pool[:, cols] + with_prv * rows_r[0, :, cols] + with_nxt * rows_r[1, :, cols]) * inv_len
        pool[:, cols] = p
        norms.append(jnp.sum(p * p, axis=1, keepdims=True))
        inners.append(jnp.sum(p * tokc[:, cols], axis=1, keepdims=True))

    rc = iota((256, T), 0)
    tc = iota((256, T), 1)
    doc_of = ((rc >> 4) & 3) * 16 + (rc >> 6) * 4 + (rc & 3)
    at_a = pick(doc_of == tc, starts, 1) - base == tc.astype(F32)
    part = (rc >> 2) & 3
    for h in range(2):
        total = None
        for c in range(4):
            hot = jnp.where(jnp.logical_and(at_a, part == c), 1.0, 0.0).astype(BF16)
            term = dot(hot, pool[:, c * C + h * 512 : c * C + (h + 1) * 512].astype(BF16))
            total = term if total is None else total + term
        s2[:, h * 512 : (h + 1) * 512] = total.astype(BF16)

    def px_copy(i):
        return remote(
            s2.at[rows_of(((x + i) % NX) * 64, 64)], rx.at[x], px_snd.at[i], px_rcv.at[x], at_x(i)
        )

    def px_wait(i):
        return remote(s2.at[rows_of(x * 64, 64)], rx.at[(x + i) % NX], px_snd.at[i], px_rcv.at[(x + i) % NX], at_x(i))

    for i in range(1, NX):
        px_copy(i).start()

    def pb_copy(c):
        return remote(s2b.at[rows_of((c - HALF) * 16, 16)], rb, pb_snd.at[c - HALF], pb_rcv.at[0], (dp, c))

    @pl.when(ctx == LAST)
    def _():
        doc_of = 64 + (rc >> 4) * 4 + (rc & 3)
        at_b = pick(doc_of == tc, starts, 1) - base == tc.astype(F32)
        for h in range(2):
            total = None
            for c in range(4):
                hot = jnp.where(jnp.logical_and(at_b, part == c), 1.0, 0.0).astype(BF16)
                term = dot(hot, pool[:, c * C + h * 512 : c * C + (h + 1) * 512].astype(BF16))
                total = term if total is None else total + term
            s2b[:, h * 512 : (h + 1) * 512] = total.astype(BF16)

        @pl.loop(HALF, LAST)
        def _(c):
            pb_copy(c).start()

    by_quarter = [norms[2 * c] + norms[2 * c + 1] for c in range(4)]
    inner_quarter = [inners[2 * c] + inners[2 * c + 1] for c in range(4)]
    n1 = by_quarter[0]
    n2 = n1 + by_quarter[1]
    n4 = n2 + by_quarter[2] + by_quarter[3]
    d1 = inner_quarter[0]
    d2 = d1 + inner_quarter[1]
    d4 = d2 + inner_quarter[2] + inner_quarter[3]
    i1, i2, i4 = lax.rsqrt(n1 + EPS), lax.rsqrt(n2 + EPS), lax.rsqrt(n4 + EPS)
    b1, b2, b4 = i1 * i1 * i1 * d1, i2 * i2 * i2 * d2, i4 * i4 * i4 * d4
    left = [i1 + i2 + i4, i2 + i4, i4, i4]
    right = [b1 + b2 + b4, b2 + b4, b4, b4]
    for c in range(8):
        cols = slice(c * 512, (c + 1) * 512)
        ga[:, cols] = ((left[c // 2] * tokc[:, cols] - right[c // 2] * pool[:, cols]) * inv_len).astype(BF16)

    def grad_copy(g, i):
        return remote(
            dh_s.at[g, i], dh_r.at[g, i], d_snd.at[g, i], d_rcv.at[g, i], (dp, prv if i % 2 == 0 else nxt)
        )

    def backward(g, carry):
        q_sum, k_sum = carry
        for p in range(R):
            cols = cols_of(g * (R * T) + p * T, T)
            rows = slice(p * T, (p + 1) * T)
            do = ga[:, cols]
            dos[rows, :] = do
            probs = pr[g, rows, :]
            dprobs = dot(do, vw[g], NT)
            inner = jnp.sum(probs * dprobs, axis=-1, keepdims=True)
            ds = (probs * (dprobs - inner)).astype(BF16)
            dss[rows, :] = ds
            lows[rows, :] = probs.astype(BF16)
            dq = dot(ds, kn[g]) * SCALE
            unit = uq[g, rows, :]
            q_sum = q_sum + jnp.sum(dq * unit, axis=0, keepdims=True)
            scaled = dq * q_gain
            mean = jnp.mean(scaled * unit, axis=-1, keepdims=True)
            gq_ref[:, cols] = (iq[g, rows, :] * (scaled - unit * mean)).astype(BF16)
        dk = dot(dss[...], qn[g], TN) * SCALE
        dv = dot(lows[...], dos[...], TN)
        k_sum = k_sum + jnp.sum(dk * uk[g], axis=0, keepdims=True)
        dh_s[g, 0] = dk[:T].astype(BF16)
        dh_s[g, 1] = dk[2 * T :].astype(BF16)
        dh_s[g, 2] = dv[:T].astype(BF16)
        dh_s[g, 3] = dv[2 * T :].astype(BF16)
        for i in range(4):
            grad_copy(g, i).start()
        dk_own[g] = dk[T : 2 * T]
        dv_own[g] = dv[T : 2 * T]
        return q_sum, k_sum

    zero = jnp.zeros((1, T), F32)
    sums = lax.fori_loop(0, G // 2, backward, (zero, zero))

    def pz_copy(i):
        return remote(
            zs.at[rows_of(((z + i) % NZ) * 16, 16)], rz.at[z], pz_snd.at[i], pz_rcv.at[z], at_z(i)
        )

    def pz_wait(i):
        return remote(zs.at[rows_of(0, 16)], rz.at[(z + i) % NZ], pz_snd.at[i], pz_rcv.at[(z + i) % NZ], at_z(i))

    def to_low(i):
        return (z + i) % NZ < NZ // 2

    for i in range(1, NX):
        px_wait(i).wait_recv()
    merged = s2[rows_of(x * 64, 64), :].astype(F32)
    for i in range(1, NX):
        merged = merged + rx[(x + i) % NX].astype(F32)
    zs[...] = merged.astype(BF16)
    for i in range(1, NZ):
        @pl.when(to_low(i))
        def _():
            pz_copy(i).start()

    q_sum, k_sum = lax.fori_loop(G // 2, G, backward, sums)

    def total_of(slots, place, count, copies):
        for copy in copies:
            copy[0].start()
        for copy in copies:
            copy[1].wait_recv()
        total = slots[0]
        for i in range(1, count):
            total = total + slots[i]
        return total

    def gain_pair(slots, snd, rcv, i, place, other, device):
        return (
            remote(slots.at[place], slots.at[place], snd.at[i], rcv.at[place], device),
            remote(slots.at[other], slots.at[other], snd.at[i], rcv.at[other], device),
        )

    r8 = iota((8, T), 0)
    gz[z] = jnp.where(r8 == 0, q_sum, jnp.where(r8 == 1, k_sum, 0.0))
    z_pairs = [gain_pair(gz, gz_snd, gz_rcv, i, z, (z + i) % NZ, at_z(i)) for i in range(1, NZ)]
    gy[y] = total_of(gz, z, NZ, z_pairs)
    y_pairs = [gain_pair(gy, gy_snd, gy_rcv, i, y, (y + i) % ny, at_y(i)) for i in range(1, ny)]
    spot = core * NX + x
    gx[spot] = total_of(gy, y, ny, y_pairs)
    x_pairs = []
    for j in range(nc):
        for i in range(NX):
            if i or j:
                there = (core + j) % nc
                other = there * NX + (x + i) % NX
                device = (y * nc + there, z * NX + (x + i) % NX)
                x_pairs.append(gain_pair(gx, gx_snd, gx_rcv, j * NX + i, spot, other, device))
    total = total_of(gx, spot, NX * nc, x_pairs)
    qgain_ref[...] = total[0:1]
    kgain_ref[...] = total[1:2]

    @pl.loop(0, G)
    def _(g):
        for i in range(4):
            grad_copy(g, i).wait_recv()
        cols = cols_of(g * T, T)
        dk = dk_own[g] + (dh_r[g, 0].astype(F32) + dh_r[g, 1].astype(F32))
        dv = dv_own[g] + (dh_r[g, 2].astype(F32) + dh_r[g, 3].astype(F32))
        unit = uk[g, T : 2 * T, :]
        scaled = dk * k_gain
        mean = jnp.mean(scaled * unit, axis=-1, keepdims=True)
        gk_ref[:, cols] = (ik[g] * (scaled - unit * mean)).astype(BF16)
        gv_ref[:, cols] = dv.astype(BF16)

    def embed(rows):
        parts = [rows[c * 4 : c * 4 + 4] for c in range(4)]
        squares = [jnp.sum(part * part, axis=1, keepdims=True) for part in parts]
        m1 = squares[0]
        m2 = m1 + squares[1]
        m4 = m2 + squares[2] + squares[3]
        eq_ref[...] = parts[0] * lax.rsqrt(m1 + EPS)
        for ref, m, count in ((eh_ref, m2, 2), (ef_ref, m4, 4)):
            inv = lax.rsqrt(m + EPS)
            for c in range(count):
                ref[:, c * C : (c + 1) * C] = parts[c] * inv

    @pl.when(low_half)
    def _():
        rows = zs[rows_of(z * 16, 16), :].astype(F32)
        for i in range(1, NZ):
            pz_wait(i).wait_recv()
            rows = rows + rz[(z + i) % NZ].astype(F32)
        embed(rows)

    @pl.when(sends_b)
    def _():
        pb_copy(ctx).wait_recv()
        embed(rb[...].astype(F32))

    @pl.when(ctx == LAST)
    def _():
        embed(s2b[(HALF - 1) * 16 : HALF * 16, :].astype(F32))

    @pl.loop(0, G)
    def _(g):
        for i in range(4):
            halo_copy(g, i).wait_send()
            grad_copy(g, i).wait_send()
    row_copy(0).wait_send()
    row_copy(1).wait_send()
    for i in range(1, NX):
        cx_copy(i).wait_send()
        px_copy(i).wait_send()
    for i in range(1, NZ):
        @pl.when(low_half)
        def _():
            cz_copy(i).wait_send()

        @pl.when(to_low(i))
        def _():
            pz_copy(i).wait_send()

    @pl.when(sends_b)
    def _():
        cb_copy(ctx).wait_send()

    @pl.when(ctx == LAST)
    def _():
        @pl.loop(HALF, LAST)
        def _(c):
            pb_copy(c).wait_send()
    for pair in z_pairs + y_pairs + x_pairs:
        pair[0].wait_send()


def body(queries, keys, values, doc_lengths, cotangent, query_gain, key_gain):
    nc = 2 if lax.axis_size("dp") > 1 else 1
    ny = lax.axis_size("dp") // nc
    vmem, dma = pltpu.VMEM, pltpu.SemaphoreType.DMA
    scratch = [
        vmem((G, 4, T, T), BF16),
        vmem((G, 3 * T, T), BF16),
        vmem((G, 3 * T, T), F32),
        vmem((G, T, 1), F32),
        vmem((G, 3 * T, T), BF16),
        vmem((G, R * T, T), BF16),
        vmem((G, R * T, T), F32),
        vmem((G, R * T, 1), F32),
        vmem((G, R * T, 3 * T), F32),
        vmem((T, 3 * T), F32),
        vmem((T, W), BF16),
        vmem((T, W), F32),
        vmem((T, W), F32),
        vmem((T, W), BF16),
        vmem((2, 1, W), F32),
        vmem((2, 1, W), F32),
        vmem((16, C), F32),
        vmem((16, C), BF16),
        vmem((256, C), BF16),
        vmem((256, C), BF16),
        vmem((256, C), BF16),
        vmem((256, C), BF16),
        vmem((NX, 64, C), BF16),
        vmem((64, C), BF16),
        vmem((NZ, 16, C), BF16),
        vmem((16, C), BF16),
        vmem((R * T, 3 * T), BF16),
        vmem((R * T, 3 * T), BF16),
        vmem((R * T, T), BF16),
        vmem((G, 4, T, T), BF16),
        vmem((G, 4, T, T), BF16),
        vmem((G, T, T), F32),
        vmem((G, T, T), F32),
        vmem((NZ, 8, T), F32),
        vmem((ny, 8, T), F32),
        vmem((nc * NX, 8, T), F32),
        dma((G, 4)), dma((G, 4)),
        dma((2,)), dma((2,)),
        dma((NZ,)), dma((NZ,)),
        dma((NX,)), dma((NX,)),
        dma((1,)), dma((HALF,)),
        dma((NX,)), dma((NX,)),
        dma((NZ,)), dma((NZ,)),
        dma((HALF,)), dma((1,)),
        dma((G, 4)), dma((G, 4)),
        dma((NZ,)), dma((NZ,)),
        dma((ny,)), dma((ny,)),
        dma((nc * NX,)), dma((nc * NX,)),
    ]
    shape = jax.ShapeDtypeStruct
    outs = pl.pallas_call(
        functools.partial(kernel, ny, nc),
        out_shape=(
            shape((4, C), F32),
            shape((4, 2 * C), F32),
            shape((4, W), F32),
            shape((T, W), BF16),
            shape((T, G * T), BF16),
            shape((T, G * T), BF16),
            shape((1, T), F32),
            shape((1, T), F32),
        ),
        in_specs=[pl.BlockSpec(memory_space=pltpu.VMEM)] * 7,
        out_specs=tuple([pl.BlockSpec(memory_space=pltpu.VMEM)] * 8),
        scratch_shapes=scratch,
        compiler_params=pltpu.CompilerParams(
            collective_id=0, has_side_effects=True, vmem_limit_bytes=56 * 1024 * 1024
        ),
    )(
        queries[0], keys[0], values[0], doc_lengths, cotangent[0],
        query_gain.reshape(1, T), key_gain.reshape(1, T),
    )
    eq, eh, ef, gq, gk, gv, qgain, kgain = outs
    return (eq[None], eh[None], ef[None], gq[None], gk[None], gv[None], qgain[0], kgain[0])


def solution(mesh):
    rows = P("dp", "ctx", None)
    in_specs = (rows, rows, rows, P("dp", None), rows, P(), P())
    out_specs = (rows, rows, rows, rows, rows, rows, P(), P())
    return jax.shard_map(body, mesh=mesh, in_specs=in_specs, out_specs=out_specs, check_vma=False)
```

time: 841 us -> 99.4 us (0.12)
  waiting for transfers between devices: 447 us -> 0 us
  blocking collectives: 102 us -> 0 us
  Pallas kernels: 0 us -> 89.8 us
  local copies, waits for them, and re-layouts: 92.7 us -> 8.64 us
  matrix products: 77.2 us -> 0 us
  starting transfers between devices: 63.1 us -> 0 us
  other arithmetic: 29.8 us -> 0 us
  between operations: 15.2 us -> 0.66 us
  loops' own time: 11.5 us -> 0 us
    all_to_all x8 -> x0, waiting for transfers between devices: 207 us -> none  [the longest x1 40.4 us: body(): lax.all_to_all(grad_head_v.reshape(total, local_heads * width), 'ctx', sp...]
    unnamed x3 -> x0, waiting for transfers between devices: 160 us -> none
    psum x1 -> x0, blocking collectives: 102 us -> none  [body(): total_qgain, total_kgain = lax.psum((grad_qgain, grad_kgain), ('dp', 'ctx'))]
    pallas_call x0 -> x1, Pallas kernels: none -> 89.8 us  [body(): pl.pallas_call(functools.partial(kernel, ny, nc), out_shape=(shape((4, C)...]
    all_gather x1 -> x0, waiting for transfers between devices: 79.2 us -> none  [spread_tokens(): lax.all_gather(scaled.astype(jnp.bfloat16), 'ctx', axis=0, tiled=True)]
    dot_general x57 -> x0, matrix products: 77.2 us -> none  [the longest x16 22.2 us: block_probs(): jnp.einsum('rgpe,kge->gprk', grouped, keys, preferred_element_type=jnp.fl...]
    all_to_all x8 -> x0, starting transfers between devices: 63.1 us -> none  [the longest x1 13.7 us: body(): lax.all_to_all(value_rep, 'ctx', split_axis=1, concat_axis=0, tiled=True)]
    dynamic_slice x80 -> x0, local copies, waits for them, and re-layouts: 30.8 us -> none  [the longest x16 9.53 us: backward(): lax.dynamic_slice_in_dim(key_acc, start, window, 0) + grad_k]
  transfers between devices with their start and end apart: 10 -> 0, of which waited for: 10 -> 0; matrix products, arithmetic and copies ran while one was open for 3% -> 0% of each run, Pallas kernels for 0% -> 0%
where the time goes in v1:
time: 99.4 us; the launch traced here: 99.1 us
  Pallas kernels  89.8 us (90%)
  local copies, waits for them, and re-layouts  8.64 us (9%)
    pallas_call x1, Pallas kernels, body(): pl.pallas_call(functools.partial(kernel, ny, nc), out_shape=(shape((4, C)...  89.8 us
    unnamed x18, local copies, waits for them, and re-layouts  8.64 us

profile of v1, /device:TPU:1, one launch (start us, length us, event | category | flops | bytes accessed | tf_op | source)
XLA Modules:
  0.0 99.1 jit_solution(18010687738484250354)
XLA Ops:
  0.6 89.8 %shard_map.134 = (f32[4,1024]{1,0:T(4,128)}, f32[4,2048]{1,0:T(4,128)}, f32[4,4096]{1,0:T(4,128)}, bf16[128,4096]{1,0:T(8,128)(2,1)}, bf16[128,1024]{1,0:T(8,128...) custom-call(bf16[128,4096]{1,0:T(8,128)(2,1)} %bitcast.14, bf16[128,1024]{1,0:T(8,128)(2,1)} %bitcast.18, ...), custom_call_target="tpu_custom_call" | custom-call | tf_op jit(solution)/shard_map/pallas_call | solution.py:575
  90.4 0.0 copy-start.2
  90.4 1.4 %copy.23 = f32[1,4,1024]{2,1,0:T(4,128)} copy(f32[1,4,1024]{2,1,0:T(4,128)} %bitcast.23) | data formatting | bytes 32768
  91.8 1.4 %copy.24 = f32[1,4,2048]{2,1,0:T(4,128)} copy(f32[1,4,2048]{2,1,0:T(4,128)} %bitcast.22) | data formatting | bytes 65536
  93.1 0.0 copy-done.2
  93.1 0.6 copy.25
  93.8 0.0 copy-start.1
  93.8 2.3 %copy.26 = bf16[1,128,4096]{2,1,0:T(8,128)(2,1)} copy(bf16[1,128,4096]{2,1,0:T(8,128)(2,1)} %bitcast.15) | data formatting | bytes 2097152
  96.1 0.0 copy-done.1
  96.1 0.0 copy-start
  96.1 0.7 copy.27
  96.8 0.3 copy-done
  97.1 0.0 copy-start.4
  97.1 0.7 copy.28
  97.9 0.0 copy-done.4
  97.9 0.0 copy-start.3
  97.9 0.5 copy.29
  98.4 0.2 copy-done.3
  98.5 0.5 copy.30
Async XLA Ops:
  90.4 2.7 %copy-start.2 = (f32[4,4096]{1,0:T(4,128)S(1)}, f32[4,4096]{1,0:T(4,128)}, u32[]{:S(2)}) copy-start(f32[4,4096]{1,0:T(4,128)} %get-tuple-element.18) | copy-start | bytes 196612
  93.8 2.3 %copy-start.1 = (bf16[128,1024]{1,0:T(8,128)(2,1)S(1)}, bf16[128,1024]{1,0:T(8,128)(2,1)}, u32[]{:S(2)}) copy-start(bf16[128,1024]{1,0:T(8,128)(2,1)} %get-tuple-element.20) | copy-start | bytes 786436
  96.1 1.0 %copy-start = (bf16[128,1024]{1,0:T(8,128)(2,1)S(1)}, bf16[128,1024]{1,0:T(8,128)(2,1)}, u32[]{:S(2)}) copy-start(bf16[128,1024]{1,0:T(8,128)(2,1)} %get-tuple-element.21) | copy-start | bytes 786436
  97.1 0.7 copy-start.4
  97.9 0.7 copy-start.3

commit v2 on v1

v2 whole, which is shorter than its diff:
```python
import functools
import math

import jax
import jax.numpy as jnp
from jax import lax
from jax.experimental import pallas as pl
from jax.experimental.pallas import tpu as pltpu
from jax.sharding import PartitionSpec as P

EPS = 1e-06
T = 128
G = 8
R = 4
W = 4096
NX, NZ = 4, 8
C = 1024
SCALE = 1.0 / math.sqrt(T)
LOG2E = 1.4426950408889634
NEG = -1e30
F32, BF16 = jnp.float32, jnp.bfloat16
MESH = pl.DeviceIdType.MESH
LAST = NX * NZ - 1
HALF = NX * NZ // 2
SLOTS = 9
NT = (((1,), (1,)), ((), ()))
TN = (((0,), (0,)), ((), ()))


def iota(shape, dim):
    return lax.broadcasted_iota(jnp.int32, shape, dim)


def dot(a, b, dims=(((1,), (0,)), ((), ()))):
    return lax.dot_general(a, b, dims, preferred_element_type=F32)


def rows_of(start, size):
    return pl.ds(pl.multiple_of(start, 16), size)


def cols_of(start, size):
    return pl.ds(pl.multiple_of(start, 128), size)


def kernel(
    ny, nc,
    q_ref, k_ref, v_ref, len_ref, cot_ref, qg_ref, kg_ref,
    eq_ref, eh_ref, ef_ref, gq_ref, gk_ref, gv_ref, qgain_ref, kgain_ref,
    qv, kv, vv, halo, kn, uk, ik, vw, qn, uq, iq, pr, bias, att, pool, tokc, ga, rows_s, rows_r,
    blk32, blk, cot_a, cot_b, s2, s2b, rx, zs, rz, rb, dss, lows, dos, dqs, dh_s, dh_r, dk_own, dv_own,
    gz, gy, gx,
    l_sem, h_snd, h_rcv, r_snd, r_rcv, cz_snd, cz_rcv, cx_snd, cx_rcv, cb_snd, cb_rcv,
    px_snd, px_rcv, pz_snd, pz_rcv, pb_snd, pb_rcv, d_snd, d_rcv,
    gz_snd, gz_rcv, gy_snd, gy_rcv, gx_snd, gx_rcv,
):
    dp, ctx = lax.axis_index("dp"), lax.axis_index("ctx")
    z, x = ctx // NX, ctx % NX
    y, core = dp // nc, dp % nc
    nxt, prv = (ctx + 1) % (NX * NZ), (ctx + NX * NZ - 1) % (NX * NZ)
    keeps = ctx < HALF
    sends_b = jnp.logical_and(ctx >= HALF, ctx < LAST)

    def at_z(i):
        return (dp, ((z + i) % NZ) * NX + x)

    def at_x(i):
        return (dp, z * NX + (x + i) % NX)

    def at_y(i):
        return (((y + i) % ny) * nc + core, ctx)

    loads = [
        pltpu.make_async_copy(src, dst, l_sem.at[i])
        for i, (src, dst) in enumerate(((k_ref, kv), (v_ref, vv), (q_ref, qv)))
    ]
    for load in loads:
        load.start()

    barrier = pltpu.get_barrier_semaphore()

    def greet(device):
        pl.semaphore_signal(barrier, inc=1, device_id=device, device_id_type=MESH)

    for i in range(1, NZ):
        greet(at_z(i))
    for i in range(1, NX):
        greet(at_x(i))
    for i in range(1, ny):
        greet(at_y(i))
    for j in range(1, nc):
        for i in range(NX):
            greet((y * nc + (core + j) % nc, z * NX + (x + i) % NX))

    @pl.when(x == NX - 1)
    def _():
        greet((dp, nxt))

    @pl.when(x == 0)
    def _():
        greet((dp, prv))

    @pl.when(sends_b)
    def _():
        greet((dp, LAST))

    @pl.when(ctx == LAST)
    def _():
        @pl.loop(HALF, LAST)
        def _(c):
            greet((dp, c))

    count = (NZ - 1) + (NX - 1) + (ny - 1) + NX * (nc - 1)
    edge = jnp.where(jnp.logical_or(x == 0, x == NX - 1), 1, 0)
    far = jnp.where(ctx == LAST, LAST - HALF, jnp.where(sends_b, 1, 0))
    arrivals = count + edge + far

    lens = jnp.broadcast_to(len_ref[...].astype(F32), (T, T))
    ii, jj = iota((T, T), 0), iota((T, T), 1)
    base = (ctx * T).astype(F32)

    def pick(cond, value, axis):
        return jnp.sum(jnp.where(cond, value, 0.0), axis=axis, keepdims=True)

    lens_col = pick(ii == jj, lens, 1)
    ends_col = pick(jj <= ii, lens, 1)
    ends_row = pick(ii <= jj, jnp.broadcast_to(lens_col, (T, T)), 0)
    starts = ends_row - lens[:1]
    ids_col = pick(base + ii.astype(F32) >= ends_row, 1.0, 1)
    key_pos = base - T + iota((T, 3 * T), 1).astype(F32)
    ids_row = jnp.where(key_pos[:1] < 0.0, -1.0, pick(key_pos >= ends_col, 1.0, 0))
    bias[...] = jnp.where(ids_col == ids_row, 0.0, NEG)
    own_row = ids_row[:, T : 2 * T]
    same = jnp.where(ids_col == own_row, 1.0, 0.0).astype(BF16)
    inv_len = 1.0 / pick(ids_col == jj.astype(F32), lens, 1)
    first_id = jnp.min(own_row, axis=1, keepdims=True)
    last_id = jnp.max(own_row, axis=1, keepdims=True)
    with_prv = jnp.where(ids_col == jnp.max(ids_row[:, :T], axis=1, keepdims=True), 1.0, 0.0)
    with_nxt = jnp.where(ids_col == jnp.min(ids_row[:, 2 * T :], axis=1, keepdims=True), 1.0, 0.0)
    r8 = iota((8, T), 0)
    ends8 = jnp.where(
        jnp.logical_or(
            jnp.logical_and(r8 == 0, own_row == first_id), jnp.logical_and(r8 == 1, own_row == last_id)
        ),
        1.0,
        0.0,
    ).astype(BF16)

    for c in range(4):
        blk32[c * 4 : c * 4 + 4, :] = cot_ref[:, c * C : (c + 1) * C]
    high = blk32[...].astype(BF16)
    blk[:16, :] = high
    blk[16:, :] = (blk32[...] - high.astype(F32)).astype(BF16)

    pl.semaphore_wait(barrier, arrivals)

    def remote(src, dst, snd, rcv, device):
        return pltpu.make_async_remote_copy(
            src_ref=src, dst_ref=dst, send_sem=snd, recv_sem=rcv, device_id=device, device_id_type=MESH
        )

    def halo_copy(g, i):
        src = (kv if i < 2 else vv).at[:, cols_of(g * T, T)]
        return remote(src, halo.at[g, i], h_snd.at[g, i], h_rcv.at[g, i], (dp, nxt if i % 2 == 0 else prv))

    loads[0].wait()
    loads[1].wait()

    @pl.loop(0, G)
    def _(g):
        for i in range(4):
            halo_copy(g, i).start()

    def cz_copy(zz):
        return remote(blk, cot_a.at[rows_of((ctx - zz) * 32, 32)], cz_snd.at[zz], cz_rcv.at[ctx - zz], (dp, zz * NX + x))

    def cz_wait(w):
        return remote(blk, cot_a.at[rows_of(w * 32, 32)], cz_snd.at[0], cz_rcv.at[w], at_z(1))

    def cx_copy(w, i):
        own = cot_a.at[rows_of(w * 32, 32)]
        return remote(own, own, cx_snd.at[w, i], cx_rcv.at[w], at_x(i))

    def cb_copy(c):
        return remote(blk, cot_b.at[rows_of((c - HALF) * 32, 32)], cb_snd.at[0], cb_rcv.at[c - HALF], (dp, LAST))

    first_z, last_z = jnp.maximum(ctx - (SLOTS - 1), 0), jnp.minimum(ctx, NZ - 1)
    first_w = (x + NX * NZ - z) % NX

    def each_slot(fn):
        @pl.loop(0, 3)
        def _(j):
            w = first_w + NX * j

            @pl.when(w < SLOTS)
            def _():
                fn(w)

    def each_z(fn):
        @pl.loop(first_z, last_z + 1)
        def _(zz):
            @pl.when(zz != z)
            def _():
                fn(zz)

    @pl.when(keeps)
    def _():
        @pl.when(ctx - z < SLOTS)
        def _():
            cot_a[rows_of((ctx - z) * 32, 32), :] = blk[...]
        each_z(lambda zz: cz_copy(zz).start())

    @pl.when(sends_b)
    def _():
        cb_copy(ctx).start()

    @pl.when(ctx == LAST)
    def _():
        cot_b[(HALF - 1) * 32 : HALF * 32, :] = blk[...]

    q_gain, k_gain = qg_ref[...], kg_ref[...]

    loads[2].wait()

    @pl.loop(0, G)
    def _(g):
        for p in range(R):
            rows = slice(p * T, (p + 1) * T)
            raw = qv[:, cols_of(g * (R * T) + p * T, T)].astype(F32)
            inv = lax.rsqrt(jnp.mean(raw * raw, axis=-1, keepdims=True) + EPS)
            unit = raw * inv
            uq[g, rows, :] = unit
            iq[g, rows, :] = inv
            qn[g, rows, :] = (unit * q_gain).astype(BF16)

    def forward(g):
        for i in range(4):
            halo_copy(g, i).wait_recv()
        cols = cols_of(g * T, T)
        for i, raw in enumerate((halo[g, 0], kv[:, cols], halo[g, 1])):
            raw = raw.astype(F32)
            inv = lax.rsqrt(jnp.mean(raw * raw, axis=-1, keepdims=True) + EPS)
            unit = raw * inv
            uk[g, i * T : (i + 1) * T, :] = unit
            kn[g, i * T : (i + 1) * T, :] = (unit * k_gain).astype(BF16)
            if i == 1:
                ik[g] = inv
        vw[g, :T, :] = halo[g, 2]
        vw[g, T : 2 * T, :] = vv[:, cols]
        vw[g, 2 * T :, :] = halo[g, 3]
        for p in range(R):
            rows = slice(p * T, (p + 1) * T)
            s = dot(qn[g, rows, :], kn[g], NT) * (SCALE * LOG2E) + bias[...]
            powers = jnp.exp2(s - jnp.max(s, axis=-1, keepdims=True))
            probs = powers * (1.0 / jnp.sum(powers, axis=-1, keepdims=True))
            pr[g, rows, :] = probs
            att[:, cols_of(g * (R * T) + p * T, T)] = dot(probs.astype(BF16), vw[g]).astype(BF16)

    @pl.loop(0, G // 2)
    def _(g):
        forward(g)

    def along_x(w):
        @pl.when(z + w != z * NX + x)
        def _():
            cz_wait(w).wait_recv()
        for i in range(1, NX):
            cx_copy(w, i).start()

    each_slot(along_x)

    @pl.loop(G // 2, G)
    def _(g):
        forward(g)

    for c in range(8):
        cols = slice(c * 512, (c + 1) * 512)
        ends = dot(ends8, att[:, cols])
        rows_s[0, :, cols] = ends[0:1]
        rows_s[1, :, cols] = ends[1:2]

    def row_copy(i):
        return remote(rows_s.at[i], rows_r.at[1 - i], r_snd.at[i], r_rcv.at[1 - i], (dp, prv if i == 0 else nxt))

    row_copy(0).start()
    row_copy(1).start()
    for c in range(8):
        cols = slice(c * 512, (c + 1) * 512)
        pool[:, cols] = dot(same, att[:, cols])

    @pl.loop(0, SLOTS)
    def _(w):
        @pl.when((z + w) % NX != x)
        def _():
            cx_copy(w, 1).wait_recv()

    def docs_of(count):
        rr = iota((1, count), 1)
        return ((rr >> 5) * 4 + (rr & 3)).astype(F32), (rr >> 2) & 3

    doc_a, quarter_a = docs_of(SLOTS * 32)
    doc_a = doc_a + (z * 4).astype(F32)
    doc_b, quarter_b = docs_of(HALF * 32)
    doc_b = doc_b + 4.0 * HALF
    for c in range(8):
        cols = slice((c % 2) * 512, (c % 2 + 1) * 512)
        hot = jnp.where(jnp.logical_and(ids_col == doc_a, quarter_a == c // 2), 1.0, 0.0).astype(BF16)
        tokc[:, c * 512 : (c + 1) * 512] = dot(hot, cot_a[:, cols])

    @pl.when(ctx == LAST)
    def _():
        @pl.loop(HALF, LAST)
        def _(c):
            cb_copy(c).wait_recv()
        for c in range(8):
            cols = slice((c % 2) * 512, (c % 2 + 1) * 512)
            hot = jnp.where(jnp.logical_and(ids_col == doc_b, quarter_b == c // 2), 1.0, 0.0).astype(BF16)
            tokc[:, c * 512 : (c + 1) * 512] += dot(hot, cot_b[:, cols])

    row_copy(0).wait_recv()
    row_copy(1).wait_recv()
    norms, inners = [], []
    for c in range(8):
        cols = slice(c * 512, (c + 1) * 512)
        p = (pool[:, cols] + with_prv * rows_r[0, :, cols] + with_nxt * rows_r[1, :, cols]) * inv_len
        pool[:, cols] = p
        norms.append(jnp.sum(p * p, axis=1, keepdims=True))
        inners.append(jnp.sum(p * tokc[:, cols], axis=1, keepdims=True))

    by_quarter = [norms[2 * c] + norms[2 * c + 1] for c in range(4)]
    inner_quarter = [inners[2 * c] + inners[2 * c + 1] for c in range(4)]
    n1 = by_quarter[0]
    n2 = n1 + by_quarter[1]
    n4 = n2 + by_quarter[2] + by_quarter[3]
    d1 = inner_quarter[0]
    d2 = d1 + inner_quarter[1]
    d4 = d2 + inner_quarter[2] + inner_quarter[3]
    i1, i2, i4 = lax.rsqrt(n1 + EPS), lax.rsqrt(n2 + EPS), lax.rsqrt(n4 + EPS)
    b1, b2, b4 = i1 * i1 * i1 * d1, i2 * i2 * i2 * d2, i4 * i4 * i4 * d4
    left = [i1 + i2 + i4, i2 + i4, i4, i4]
    right = [b1 + b2 + b4, b2 + b4, b4, b4]
    for c in range(8):
        cols = slice(c * 512, (c + 1) * 512)
        ga[:, cols] = ((left[c // 2] * tokc[:, cols] - right[c // 2] * pool[:, cols]) * inv_len).astype(BF16)

    def grad_copy(g, i):
        return remote(
            dh_s.at[g, i], dh_r.at[g, i], d_snd.at[g, i], d_rcv.at[g, i], (dp, prv if i % 2 == 0 else nxt)
        )

    def scores(g, carry):
        q_sum, k_sum = carry
        for p in range(R):
            rows = slice(p * T, (p + 1) * T)
            probs = pr[g, rows, :]
            dprobs = dot(ga[:, cols_of(g * (R * T) + p * T, T)], vw[g], NT)
            inner = jnp.sum(probs * dprobs, axis=-1, keepdims=True)
            ds = (probs * (dprobs - inner)).astype(BF16)
            dss[rows, :] = ds
            dq = dot(ds, kn[g]) * SCALE
            dqs[g, rows, :] = dq
            q_sum = q_sum + jnp.sum(dq * uq[g, rows, :], axis=0, keepdims=True)
        dk = dot(dss[...], qn[g], TN) * SCALE
        k_sum = k_sum + jnp.sum(dk * uk[g], axis=0, keepdims=True)
        dh_s[g, 0] = dk[:T].astype(BF16)
        dh_s[g, 1] = dk[2 * T :].astype(BF16)
        for i in range(2):
            grad_copy(g, i).start()
        dk_own[g] = dk[T : 2 * T]
        return q_sum, k_sum

    def finish(g):
        for p in range(R):
            cols = cols_of(g * (R * T) + p * T, T)
            rows = slice(p * T, (p + 1) * T)
            dos[rows, :] = ga[:, cols]
            lows[rows, :] = pr[g, rows, :].astype(BF16)
            unit = uq[g, rows, :]
            scaled = dqs[g, rows, :] * q_gain
            mean = jnp.mean(scaled * unit, axis=-1, keepdims=True)
            gq_ref[:, cols] = (iq[g, rows, :] * (scaled - unit * mean)).astype(BF16)
        dv = dot(lows[...], dos[...], TN)
        dh_s[g, 2] = dv[:T].astype(BF16)
        dh_s[g, 3] = dv[2 * T :].astype(BF16)
        for i in range(2, 4):
            grad_copy(g, i).start()
        dv_own[g] = dv[T : 2 * T]

    zero = jnp.zeros((1, T), F32)
    sums = lax.fori_loop(0, G // 2, scores, (zero, zero))

    def gathered(count, first):
        rc, tc = iota((count * 16, T), 0), iota((count * 16, T), 1)
        doc_of = first + (rc >> 4) * 4 + (rc & 3)
        here = pick(doc_of == tc, starts, 1) - base == tc.astype(F32)
        part = (rc >> 2) & 3
        hots = [jnp.where(jnp.logical_and(here, part == c), 1.0, 0.0).astype(BF16) for c in range(4)]
        halves = []
        for h in range(2):
            total = None
            for c in range(4):
                term = dot(hots[c], pool[:, c * C + h * 512 : c * C + (h + 1) * 512].astype(BF16))
                total = term if total is None else total + term
            halves.append(total.astype(BF16))
        return halves

    halves = gathered(SLOTS, z * 4)
    for h in range(2):
        s2[:, h * 512 : (h + 1) * 512] = halves[h]

    def px_copy(w):
        dst = rx.at[x, rows_of((w // NX) * 16, 16)]
        return remote(s2.at[rows_of(w * 16, 16)], dst, px_snd.at[w], px_rcv.at[x, w // NX], (dp, z * NX + (z + w) % NX))

    def px_wait(w, xx):
        dst = rx.at[xx, rows_of((w // NX) * 16, 16)]
        return remote(s2.at[rows_of(0, 16)], dst, px_snd.at[0], px_rcv.at[xx, w // NX], at_x(1))

    def other_slots(fn):
        @pl.loop(0, SLOTS)
        def _(w):
            @pl.when((z + w) % NX != x)
            def _():
                fn(w)

    other_slots(lambda w: px_copy(w).start())

    def pb_copy(c):
        return remote(s2b.at[rows_of((c - HALF) * 16, 16)], rb, pb_snd.at[c - HALF], pb_rcv.at[0], (dp, c))

    @pl.when(ctx == LAST)
    def _():
        halves = gathered(HALF, 4 * HALF)
        for h in range(2):
            s2b[:, h * 512 : (h + 1) * 512] = halves[h]

        @pl.loop(HALF, LAST)
        def _(c):
            pb_copy(c).start()

    q_sum, k_sum = lax.fori_loop(G // 2, G, scores, sums)

    def total_of(slots, count, copies):
        for copy in copies:
            copy[1].wait_recv()
        total = slots[0]
        for i in range(1, count):
            total = total + slots[i]
        return total

    def send(copies):
        for copy in copies:
            copy[0].start()

    def gain_pair(slots, snd, rcv, i, place, other, device):
        return (
            remote(slots.at[place], slots.at[place], snd.at[i], rcv.at[place], device),
            remote(slots.at[other], slots.at[other], snd.at[i], rcv.at[other], device),
        )

    r8 = iota((8, T), 0)
    gz[z] = jnp.where(r8 == 0, q_sum, jnp.where(r8 == 1, k_sum, 0.0))
    z_pairs = [gain_pair(gz, gz_snd, gz_rcv, i, z, (z + i) % NZ, at_z(i)) for i in range(1, NZ)]
    y_pairs = [gain_pair(gy, gy_snd, gy_rcv, i, y, (y + i) % ny, at_y(i)) for i in range(1, ny)]
    spot = core * NX + x
    x_pairs = []
    for j in range(nc):
        for i in range(NX):
            if i or j:
                there = (core + j) % nc
                other = there * NX + (x + i) % NX
                device = (y * nc + there, z * NX + (x + i) % NX)
                x_pairs.append(gain_pair(gx, gx_snd, gx_rcv, j * NX + i, spot, other, device))
    send(z_pairs)

    def pz_copy(w):
        src = zs.at[rows_of((w // NX) * 16, 16)]
        return remote(src, rz.at[z], pz_snd.at[w // NX], pz_rcv.at[z], (dp, z + w))

    def pz_wait(zz):
        return remote(zs.at[rows_of(0, 16)], rz.at[zz], pz_snd.at[0], pz_rcv.at[zz], at_z(1))

    def merge(w):
        rows = s2[rows_of(w * 16, 16), :].astype(F32)
        for i in range(1, NX):
            xx = (x + i) % NX
            px_wait(w, xx).wait_recv()
            rows = rows + rx[xx, rows_of((w // NX) * 16, 16), :].astype(F32)
        zs[rows_of((w // NX) * 16, 16), :] = rows.astype(BF16)

        @pl.when(z + w != ctx)
        def _():
            pz_copy(w).start()

    each_slot(merge)

    @pl.loop(0, G // 2)
    def _(g):
        finish(g)

    gy[y] = total_of(gz, NZ, z_pairs)
    send(y_pairs)

    @pl.loop(G // 2, G)
    def _(g):
        finish(g)

    gx[spot] = total_of(gy, ny, y_pairs)
    send(x_pairs)

    @pl.loop(0, G)
    def _(g):
        for i in range(4):
            grad_copy(g, i).wait_recv()
        cols = cols_of(g * T, T)
        dk = dk_own[g] + (dh_r[g, 0].astype(F32) + dh_r[g, 1].astype(F32))
        dv = dv_own[g] + (dh_r[g, 2].astype(F32) + dh_r[g, 3].astype(F32))
        unit = uk[g, T : 2 * T, :]
        scaled = dk * k_gain
        mean = jnp.mean(scaled * unit, axis=-1, keepdims=True)
        gk_ref[:, cols] = (ik[g] * (scaled - unit * mean)).astype(BF16)
        gv_ref[:, cols] = dv.astype(BF16)

    def embed(rows):
        parts = [rows[c * 4 : c * 4 + 4] for c in range(4)]
        squares = [jnp.sum(part * part, axis=1, keepdims=True) for part in parts]
        m1 = squares[0]
        m2 = m1 + squares[1]
        m4 = m2 + squares[2] + squares[3]
        eq_ref[...] = parts[0] * lax.rsqrt(m1 + EPS)
        for ref, m, count in ((eh_ref, m2, 2), (ef_ref, m4, 4)):
            inv = lax.rsqrt(m + EPS)
            for c in range(count):
                ref[:, c * C : (c + 1) * C] = parts[c] * inv

    @pl.when(keeps)
    def _():
        near = ctx - z < SLOTS
        blk32[...] = jnp.zeros_like(blk32)

        @pl.when(near)
        def _():
            blk32[...] = zs[rows_of(((ctx - z) // NX) * 16 % 48, 16), :].astype(F32)

        @pl.loop(first_z, last_z + 1)
        def _(zz):
            @pl.when(zz != z)
            def _():
                pz_wait(zz).wait_recv()
                blk32[...] += rz[zz].astype(F32)
        embed(blk32[...])

    @pl.when(sends_b)
    def _():
        pb_copy(ctx).wait_recv()
        embed(rb[...].astype(F32))

    @pl.when(ctx == LAST)
    def _():
        embed(s2b[(HALF - 1) * 16 : HALF * 16, :].astype(F32))

    total = total_of(gx, NX * nc, x_pairs)
    qgain_ref[...] = total[0:1]
    kgain_ref[...] = total[1:2]

    @pl.loop(0, G)
    def _(g):
        for i in range(4):
            halo_copy(g, i).wait_send()
            grad_copy(g, i).wait_send()
    row_copy(0).wait_send()
    row_copy(1).wait_send()

    def sent(w):
        for i in range(1, NX):
            cx_copy(w, i).wait_send()

        @pl.when(z + w != ctx)
        def _():
            pz_copy(w).wait_send()

    each_slot(sent)
    other_slots(lambda w: px_copy(w).wait_send())

    @pl.when(keeps)
    def _():
        each_z(lambda zz: cz_copy(zz).wait_send())

    @pl.when(sends_b)
    def _():
        cb_copy(ctx).wait_send()

    @pl.when(ctx == LAST)
    def _():
        @pl.loop(HALF, LAST)
        def _(c):
            pb_copy(c).wait_send()
    for pair in z_pairs + y_pairs + x_pairs:
        pair[0].wait_send()


def emit(*refs):
    srcs, dsts, held, sem = refs[:8], refs[8:16], refs[16:24], refs[24]
    moves = []
    for i in range(8):
        parts = 4 if i == 3 else 1
        size = srcs[i].shape[0] // parts
        for p in range(parts):
            at = pl.ds(p * size, size)
            n = len(moves)
            first = pltpu.make_async_copy(srcs[i].at[at], held[i].at[at], sem.at[0, n])
            moves.append((first, pltpu.make_async_copy(held[i].at[at], dsts[i].at[at], sem.at[1, n])))
    order = sorted(range(len(moves)), key=lambda n: not 3 <= n < 7)
    for n in order:
        moves[n][0].start()
    for n in order:
        moves[n][0].wait()
        moves[n][1].start()
    for n in order:
        moves[n][1].wait()


def body(queries, keys, values, doc_lengths, cotangent, query_gain, key_gain):
    nc = 2 if lax.axis_size("dp") > 1 else 1
    ny = lax.axis_size("dp") // nc
    vmem, dma = pltpu.VMEM, pltpu.SemaphoreType.DMA
    scratch = [
        vmem((T, W), BF16),
        vmem((T, G * T), BF16),
        vmem((T, G * T), BF16),
        vmem((G, 4, T, T), BF16),
        vmem((G, 3 * T, T), BF16),
        vmem((G, 3 * T, T), F32),
        vmem((G, T, 1), F32),
        vmem((G, 3 * T, T), BF16),
        vmem((G, R * T, T), BF16),
        vmem((G, R * T, T), F32),
        vmem((G, R * T, 1), F32),
        vmem((G, R * T, 3 * T), F32),
        vmem((T, 3 * T), F32),
        vmem((T, W), BF16),
        vmem((T, W), F32),
        vmem((T, W), F32),
        vmem((T, W), BF16),
        vmem((2, 1, W), F32),
        vmem((2, 1, W), F32),
        vmem((16, C), F32),
        vmem((32, C), BF16),
        vmem((SLOTS * 32, C), BF16),
        vmem((HALF * 32, C), BF16),
        vmem((SLOTS * 16, C), BF16),
        vmem((HALF * 16, C), BF16),
        vmem((NX, 48, C), BF16),
        vmem((48, C), BF16),
        vmem((NZ, 16, C), BF16),
        vmem((16, C), BF16),
        vmem((R * T, 3 * T), BF16),
        vmem((R * T, 3 * T), BF16),
        vmem((R * T, T), BF16),
        vmem((G, R * T, T), F32),
        vmem((G, 4, T, T), BF16),
        vmem((G, 4, T, T), BF16),
        vmem((G, T, T), F32),
        vmem((G, T, T), F32),
        vmem((NZ, 8, T), F32),
        vmem((ny, 8, T), F32),
        vmem((nc * NX, 8, T), F32),
        dma((3,)),
        dma((G, 4)), dma((G, 4)),
        dma((2,)), dma((2,)),
        dma((NZ,)), dma((SLOTS,)),
        dma((SLOTS, NX)), dma((SLOTS,)),
        dma((1,)), dma((HALF,)),
        dma((SLOTS,)), dma((NX, 3)),
        dma((3,)), dma((NZ,)),
        dma((HALF,)), dma((1,)),
        dma((G, 4)), dma((G, 4)),
        dma((NZ,)), dma((NZ,)),
        dma((ny,)), dma((ny,)),
        dma((nc * NX,)), dma((nc * NX,)),
    ]
    shape = jax.ShapeDtypeStruct
    outs = pl.pallas_call(
        functools.partial(kernel, ny, nc),
        out_shape=(
            shape((4, C), F32),
            shape((4, 2 * C), F32),
            shape((4, W), F32),
            shape((T, W), BF16),
            shape((T, G * T), BF16),
            shape((T, G * T), BF16),
            shape((1, T), F32),
            shape((1, T), F32),
        ),
        in_specs=[pl.BlockSpec(memory_space=pl.ANY)] * 3 + [pl.BlockSpec(memory_space=pltpu.VMEM)] * 4,
        out_specs=tuple([pl.BlockSpec(memory_space=pltpu.VMEM)] * 8),
        scratch_shapes=scratch,
        compiler_params=pltpu.CompilerParams(
            collective_id=0, has_side_effects=True, vmem_limit_bytes=56 * 1024 * 1024
        ),
    )(
        queries[0], keys[0], values[0], doc_lengths, cotangent[0],
        query_gain.reshape(1, T), key_gain.reshape(1, T),
    )
    outs = pl.pallas_call(
        emit,
        out_shape=tuple(shape(out.shape, out.dtype) for out in outs),
        in_specs=[pl.BlockSpec(memory_space=pl.ANY)] * 8,
        out_specs=tuple([pl.BlockSpec(memory_space=pl.ANY)] * 8),
        scratch_shapes=[vmem(out.shape, out.dtype) for out in outs] + [dma((2, 11))],
    )(*outs)
    eq, eh, ef, gq, gk, gv, qgain, kgain = outs
    return (eq[None], eh[None], ef[None], gq[None], gk[None], gv[None], qgain[0], kgain[0])


def solution(mesh):
    rows = P("dp", "ctx", None)
    in_specs = (rows, rows, rows, P("dp", None), rows, P(), P())
    out_specs = (rows, rows, rows, rows, rows, rows, P(), P())
    return jax.shard_map(body, mesh=mesh, in_specs=in_specs, out_specs=out_specs, check_vma=False)
```

time: 99.4 us -> 82.5 us (0.83)
  local copies, waits for them, and re-layouts: 8.64 us -> 0 us
  Pallas kernels: 89.8 us -> 81.6 us
    pallas_call x1, Pallas kernels: 89.8 us -> 79.3 us  [body(): pl.pallas_call(functools.partial(kernel, ny, nc), out_shape=(shape((4, C)...]
    unnamed x18 -> x0, local copies, waits for them, and re-layouts: 8.64 us -> none
    pallas_call x0 -> x1, Pallas kernels: none -> 2.32 us  [body(): pl.pallas_call(emit, out_shape=tuple((shape(out.shape, out.dtype) for out...]
where the time goes in v2:
time: 82.5 us; the launch traced here: 82.3 us
  Pallas kernels  81.6 us (99%)
    pallas_call x1, Pallas kernels, body(): pl.pallas_call(functools.partial(kernel, ny, nc), out_shape=(shape((4, C)...  79.3 us
    pallas_call x1, Pallas kernels, body(): pl.pallas_call(emit, out_shape=tuple((shape(out.shape, out.dtype) for out...  2.32 us

profile of v2, /device:TPU:1, one launch (start us, length us, event | category | flops | bytes accessed | tf_op | source)
XLA Modules:
  0.0 82.3 jit_solution(14443593280080763735)
XLA Ops:
  0.6 79.3 %shard_map.134 = (f32[4,1024]{1,0:T(4,128)}, f32[4,2048]{1,0:T(4,128)}, f32[4,4096]{1,0:T(4,128)}, bf16[128,4096]{1,0:T(8,128)(2,1)}, bf16[128,1024]{1,0:T(8,128...) custom-call(bf16[128,4096]{1,0:T(8,128)(2,1)} %bitcast.14, bf16[128,1024]{1,0:T(8,128)(2,1)} %bitcast.15, ...), custom_call_target="tpu_custom_call" | custom-call | tf_op jit(solution)/shard_map/pallas_call | solution.py:683
  80.0 2.3 %shard_map.135 = (f32[4,1024]{1,0:T(4,128)}, f32[4,2048]{1,0:T(4,128)}, f32[4,4096]{1,0:T(4,128)}, bf16[128,4096]{1,0:T(8,128)(2,1)}, bf16[128,1024]{1,0:T(8,128...) custom-call(f32[4,1024]{1,0:T(4,128)} %get-tuple-element.24.refs_0_, ...), custom_call_target="tpu_custom_call" | custom-call | tf_op jit(solution)/shard_map/pallas_call | solution.py:705

commit v3 on v2

--- a/solution.py
+++ b/solution.py
@@ -133,18 +133,8 @@
     own_row = ids_row[:, T : 2 * T]
     same = jnp.where(ids_col == own_row, 1.0, 0.0).astype(BF16)
     inv_len = 1.0 / pick(ids_col == jj.astype(F32), lens, 1)
-    first_id = jnp.min(own_row, axis=1, keepdims=True)
-    last_id = jnp.max(own_row, axis=1, keepdims=True)
     with_prv = jnp.where(ids_col == jnp.max(ids_row[:, :T], axis=1, keepdims=True), 1.0, 0.0)
     with_nxt = jnp.where(ids_col == jnp.min(ids_row[:, 2 * T :], axis=1, keepdims=True), 1.0, 0.0)
-    r8 = iota((8, T), 0)
-    ends8 = jnp.where(
-        jnp.logical_or(
-            jnp.logical_and(r8 == 0, own_row == first_id), jnp.logical_and(r8 == 1, own_row == last_id)
-        ),
-        1.0,
-        0.0,
-    ).astype(BF16)
 
     for c in range(4):
         blk32[c * 4 : c * 4 + 4, :] = cot_ref[:, c * C : (c + 1) * C]
@@ -248,13 +238,17 @@
         vw[g, :T, :] = halo[g, 2]
         vw[g, T : 2 * T, :] = vv[:, cols]
         vw[g, 2 * T :, :] = halo[g, 3]
+        products = dot(qn[g], kn[g], NT)
         for p in range(R):
             rows = slice(p * T, (p + 1) * T)
-            s = dot(qn[g, rows, :], kn[g], NT) * (SCALE * LOG2E) + bias[...]
+            s = products[rows] * (SCALE * LOG2E) + bias[...]
             powers = jnp.exp2(s - jnp.max(s, axis=-1, keepdims=True))
             probs = powers * (1.0 / jnp.sum(powers, axis=-1, keepdims=True))
             pr[g, rows, :] = probs
-            att[:, cols_of(g * (R * T) + p * T, T)] = dot(probs.astype(BF16), vw[g]).astype(BF16)
+            lows[g, rows, :] = probs.astype(BF16)
+        mixed = dot(lows[g], vw[g]).astype(BF16)
+        for p in range(R):
+            att[:, cols_of(g * (R * T) + p * T, T)] = mixed[p * T : (p + 1) * T]
 
     @pl.loop(0, G // 2)
     def _(g):
@@ -275,19 +269,16 @@
 
     for c in range(8):
         cols = slice(c * 512, (c + 1) * 512)
-        ends = dot(ends8, att[:, cols])
-        rows_s[0, :, cols] = ends[0:1]
-        rows_s[1, :, cols] = ends[1:2]
+        sums = dot(same, att[:, cols])
+        pool[:, cols] = sums
+        rows_s[0, :, cols] = sums[:1]
+        rows_s[1, :, cols] = sums[T - 1 :]
 
     def row_copy(i):
         return remote(rows_s.at[i], rows_r.at[1 - i], r_snd.at[i], r_rcv.at[1 - i], (dp, prv if i == 0 else nxt))
 
     row_copy(0).start()
     row_copy(1).start()
-    for c in range(8):
-        cols = slice(c * 512, (c + 1) * 512)
-        pool[:, cols] = dot(same, att[:, cols])
-
     @pl.loop(0, SLOTS)
     def _(w):
         @pl.when((z + w) % NX != x)
@@ -302,20 +293,26 @@
     doc_a = doc_a + (z * 4).astype(F32)
     doc_b, quarter_b = docs_of(HALF * 32)
     doc_b = doc_b + 4.0 * HALF
-    for c in range(8):
-        cols = slice((c % 2) * 512, (c % 2 + 1) * 512)
-        hot = jnp.where(jnp.logical_and(ids_col == doc_a, quarter_a == c // 2), 1.0, 0.0).astype(BF16)
-        tokc[:, c * 512 : (c + 1) * 512] = dot(hot, cot_a[:, cols])
+    def spread(doc, quarter, blocks, add):
+        hits = ids_col == doc
+        hot = jnp.concatenate(
+            [jnp.where(jnp.logical_and(hits, quarter == c), 1.0, 0.0).astype(BF16) for c in range(4)], axis=0
+        )
+        for h in range(4):
+            term = dot(hot, blocks[:, h * 256 : (h + 1) * 256])
+            for c in range(4):
+                cols = slice(c * C + h * 256, c * C + (h + 1) * 256)
+                rows = term[c * T : (c + 1) * T]
+                tokc[:, cols] = tokc[:, cols] + rows if add else rows
+
+    spread(doc_a, quarter_a, cot_a, False)
 
     @pl.when(ctx == LAST)
     def _():
         @pl.loop(HALF, LAST)
         def _(c):
             cb_copy(c).wait_recv()
-        for c in range(8):
-            cols = slice((c % 2) * 512, (c % 2 + 1) * 512)
-            hot = jnp.where(jnp.logical_and(ids_col == doc_b, quarter_b == c // 2), 1.0, 0.0).astype(BF16)
-            tokc[:, c * 512 : (c + 1) * 512] += dot(hot, cot_b[:, cols])
+        spread(doc_b, quarter_b, cot_b, True)
 
     row_copy(0).wait_recv()
     row_copy(1).wait_recv()
@@ -351,15 +348,16 @@
     def scores(g, carry):
         q_sum, k_sum = carry
         for p in range(R):
+            dos[p * T : (p + 1) * T, :] = ga[:, cols_of(g * (R * T) + p * T, T)]
+        products = dot(dos[...], vw[g], NT)
+        for p in range(R):
             rows = slice(p * T, (p + 1) * T)
-            probs = pr[g, rows, :]
-            dprobs = dot(ga[:, cols_of(g * (R * T) + p * T, T)], vw[g], NT)
+            probs, dprobs = pr[g, rows, :], products[rows]
             inner = jnp.sum(probs * dprobs, axis=-1, keepdims=True)
-            ds = (probs * (dprobs - inner)).astype(BF16)
-            dss[rows, :] = ds
-            dq = dot(ds, kn[g]) * SCALE
-            dqs[g, rows, :] = dq
-            q_sum = q_sum + jnp.sum(dq * uq[g, rows, :], axis=0, keepdims=True)
+            dss[rows, :] = (probs * (dprobs - inner)).astype(BF16)
+        dq = dot(dss[...], kn[g]) * SCALE
+        dqs[g] = dq
+        q_sum = q_sum + jnp.sum(dq * uq[g], axis=0, keepdims=True)
         dk = dot(dss[...], qn[g], TN) * SCALE
         k_sum = k_sum + jnp.sum(dk * uk[g], axis=0, keepdims=True)
         dh_s[g, 0] = dk[:T].astype(BF16)
@@ -374,12 +372,11 @@
             cols = cols_of(g * (R * T) + p * T, T)
             rows = slice(p * T, (p + 1) * T)
             dos[rows, :] = ga[:, cols]
-            lows[rows, :] = pr[g, rows, :].astype(BF16)
             unit = uq[g, rows, :]
             scaled = dqs[g, rows, :] * q_gain
             mean = jnp.mean(scaled * unit, axis=-1, keepdims=True)
             gq_ref[:, cols] = (iq[g, rows, :] * (scaled - unit * mean)).astype(BF16)
-        dv = dot(lows[...], dos[...], TN)
+        dv = dot(lows[g], dos[...], TN)
         dh_s[g, 2] = dv[:T].astype(BF16)
         dh_s[g, 3] = dv[2 * T :].astype(BF16)
         for i in range(2, 4):
@@ -655,7 +652,7 @@
         vmem((NZ, 16, C), BF16),
         vmem((16, C), BF16),
         vmem((R * T, 3 * T), BF16),
-        vmem((R * T, 3 * T), BF16),
+        vmem((G, R * T, 3 * T), BF16),
         vmem((R * T, T), BF16),
         vmem((G, R * T, T), F32),
         vmem((G, 4, T, T), BF16),

time: 82.5 us -> 78.9 us (0.956)
  Pallas kernels: 81.6 us -> 78.1 us
    pallas_call x1, Pallas kernels: 79.3 us -> 75.8 us  [body(): pl.pallas_call(functools.partial(kernel, ny, nc), out_shape=(shape((4, C)...]
where the time goes in v3:
time: 78.9 us; the launch traced here: 78.7 us
  Pallas kernels  78.1 us (99%)
    pallas_call x1, Pallas kernels, body(): pl.pallas_call(functools.partial(kernel, ny, nc), out_shape=(shape((4, C)...  75.8 us
    pallas_call x1, Pallas kernels, body(): pl.pallas_call(emit, out_shape=tuple((shape(out.shape, out.dtype) for out...  2.32 us

profile of v3, /device:TPU:1, one launch (start us, length us, event | category | flops | bytes accessed | tf_op | source)
XLA Modules:
  0.0 78.7 jit_solution(1877528098678740735)
XLA Ops:
  0.6 75.8 %shard_map.134 = (f32[4,1024]{1,0:T(4,128)}, f32[4,2048]{1,0:T(4,128)}, f32[4,4096]{1,0:T(4,128)}, bf16[128,4096]{1,0:T(8,128)(2,1)}, bf16[128,1024]{1,0:T(8,128...) custom-call(bf16[128,4096]{1,0:T(8,128)(2,1)} %bitcast.14, bf16[128,1024]{1,0:T(8,128)(2,1)} %bitcast.15, ...), custom_call_target="tpu_custom_call" | custom-call | tf_op jit(solution)/shard_map/pallas_call | solution.py:680
  76.4 2.3 %shard_map.135 = (f32[4,1024]{1,0:T(4,128)}, f32[4,2048]{1,0:T(4,128)}, f32[4,4096]{1,0:T(4,128)}, bf16[128,4096]{1,0:T(8,128)(2,1)}, bf16[128,1024]{1,0:T(8,128...) custom-call(f32[4,1024]{1,0:T(4,128)} %get-tuple-element.24.refs_0_, ...), custom_call_target="tpu_custom_call" | custom-call | tf_op jit(solution)/shard_map/pallas_call | solution.py:702

commit v4 on v3

--- a/solution.py
+++ b/solution.py
@@ -47,10 +47,10 @@
     ny, nc,
     q_ref, k_ref, v_ref, len_ref, cot_ref, qg_ref, kg_ref,
     eq_ref, eh_ref, ef_ref, gq_ref, gk_ref, gv_ref, qgain_ref, kgain_ref,
-    qv, kv, vv, halo, kn, uk, ik, vw, qn, uq, iq, pr, bias, att, pool, tokc, ga, rows_s, rows_r,
+    qv, kv, vv, halo, kn, uk, ik, vw, qn, uq, iq, pr, bias, pool, tokc, ga, rows_s, rows_r,
     blk32, blk, cot_a, cot_b, s2, s2b, rx, zs, rz, rb, dss, lows, dos, dqs, dh_s, dh_r, dk_own, dv_own,
     gz, gy, gx,
-    l_sem, h_snd, h_rcv, r_snd, r_rcv, cz_snd, cz_rcv, cx_snd, cx_rcv, cb_snd, cb_rcv,
+    l_sem, h_snd, h_rcv, r_snd, r_rcv, cz_snd, cz_rcv, cx_snd, cx_rcv, cf_snd, cf_rcv, cb_snd, cb_rcv,
     px_snd, px_rcv, pz_snd, pz_rcv, pb_snd, pb_rcv, d_snd, d_rcv,
     gz_snd, gz_rcv, gy_snd, gy_rcv, gx_snd, gx_rcv,
 ):
@@ -170,6 +170,17 @@
     def cx_copy(w, i):
         own = cot_a.at[rows_of(w * 32, 32)]
         return remote(own, own, cx_snd.at[w, i], cx_rcv.at[w], at_x(i))
+
+    def cf_copy(w, h):
+        part = cot_a.at[rows_of(w * 32 + 16 * h, 16)]
+        return remote(part, part, cf_snd.at[w], cf_rcv.at[w, h], at_x(1 if h == 0 else NX - 1))
+
+    def by_column(i, fn):
+        @pl.loop(0, SLOTS)
+        def _(w):
+            @pl.when((z + w) % NX == (x + i) % NX)
+            def _():
+                fn(w)
 
     def cb_copy(c):
         return remote(blk, cot_b.at[rows_of((c - HALF) * 32, 32)], cb_snd.at[0], cb_rcv.at[c - HALF], (dp, LAST))
@@ -248,7 +259,11 @@
             lows[g, rows, :] = probs.astype(BF16)
         mixed = dot(lows[g], vw[g]).astype(BF16)
         for p in range(R):
-            att[:, cols_of(g * (R * T) + p * T, T)] = mixed[p * T : (p + 1) * T]
+            cols = cols_of(g * (R * T) + p * T, T)
+            sums = dot(same, mixed[p * T : (p + 1) * T])
+            pool[:, cols] = sums
+            rows_s[0, :, cols] = sums[:1]
+            rows_s[1, :, cols] = sums[T - 1 :]
 
     @pl.loop(0, G // 2)
     def _(g):
@@ -258,7 +273,7 @@
         @pl.when(z + w != z * NX + x)
         def _():
             cz_wait(w).wait_recv()
-        for i in range(1, NX):
+        for i in (1, NX - 1):
             cx_copy(w, i).start()
 
     each_slot(along_x)
@@ -267,23 +282,23 @@
     def _(g):
         forward(g)
 
-    for c in range(8):
-        cols = slice(c * 512, (c + 1) * 512)
-        sums = dot(same, att[:, cols])
-        pool[:, cols] = sums
-        rows_s[0, :, cols] = sums[:1]
-        rows_s[1, :, cols] = sums[T - 1 :]
-
     def row_copy(i):
         return remote(rows_s.at[i], rows_r.at[1 - i], r_snd.at[i], r_rcv.at[1 - i], (dp, prv if i == 0 else nxt))
 
     row_copy(0).start()
     row_copy(1).start()
-    @pl.loop(0, SLOTS)
-    def _(w):
-        @pl.when((z + w) % NX != x)
-        def _():
-            cx_copy(w, 1).wait_recv()
+    def pass_on(w, h):
+        cx_copy(w, 1).wait_recv()
+        cf_copy(w, h).start()
+
+    by_column(NX - 1, lambda w: pass_on(w, 0))
+    by_column(1, lambda w: pass_on(w, 1))
+
+    def passed(w):
+        for h in range(2):
+            cf_copy(w, h).wait_recv()
+
+    by_column(2, passed)
 
     def docs_of(count):
         rr = iota((1, count), 1)
@@ -323,6 +338,55 @@
         pool[:, cols] = p
         norms.append(jnp.sum(p * p, axis=1, keepdims=True))
         inners.append(jnp.sum(p * tokc[:, cols], axis=1, keepdims=True))
+
+    def gathered(count, first):
+        rc, tc = iota((count * 16, T), 0), iota((count * 16, T), 1)
+        doc_of = first + (rc >> 4) * 4 + (rc & 3)
+        here = pick(doc_of == tc, starts, 1) - base == tc.astype(F32)
+        part = (rc >> 2) & 3
+        hots = [jnp.where(jnp.logical_and(here, part == c), 1.0, 0.0).astype(BF16) for c in range(4)]
+        halves = []
+        for h in range(2):
+            total = None
+            for c in range(4):
+                term = dot(hots[c], pool[:, c * C + h * 512 : c * C + (h + 1) * 512].astype(BF16))
+                total = term if total is None else total + term
+            halves.append(total.astype(BF16))
+        return halves
+
+    halves = gathered(SLOTS, z * 4)
+    for h in range(2):
+        s2[:, h * 512 : (h + 1) * 512] = halves[h]
+
+    def px_copy(w):
+        dst = rx.at[x, rows_of((w // NX) * 16, 16)]
+        return remote(s2.at[rows_of(w * 16, 16)], dst, px_snd.at[w], px_rcv.at[x, w // NX], (dp, z * NX + (z + w) % NX))
+
+    def px_wait(w, xx):
+        dst = rx.at[xx, rows_of((w // NX) * 16, 16)]
+        return remote(s2.at[rows_of(0, 16)], dst, px_snd.at[0], px_rcv.at[xx, w // NX], at_x(1))
+
+    def other_slots(fn):
+        @pl.loop(0, SLOTS)
+        def _(w):
+            @pl.when((z + w) % NX != x)
+            def _():
+                fn(w)
+
+    other_slots(lambda w: px_copy(w).start())
+
+    def pb_copy(c):
+        return remote(s2b.at[rows_of((c - HALF) * 16, 16)], rb, pb_snd.at[c - HALF], pb_rcv.at[0], (dp, c))
+
+    @pl.when(ctx == LAST)
+    def _():
+        halves = gathered(HALF, 4 * HALF)
+        for h in range(2):
+            s2b[:, h * 512 : (h + 1) * 512] = halves[h]
+
+        @pl.loop(HALF, LAST)
+        def _(c):
+            pb_copy(c).start()
 
     by_quarter = [norms[2 * c] + norms[2 * c + 1] for c in range(4)]
     inner_quarter = [inners[2 * c] + inners[2 * c + 1] for c in range(4)]
@@ -384,58 +448,7 @@
         dv_own[g] = dv[T : 2 * T]
 
     zero = jnp.zeros((1, T), F32)
-    sums = lax.fori_loop(0, G // 2, scores, (zero, zero))
-
-    def gathered(count, first):
-        rc, tc = iota((count * 16, T), 0), iota((count * 16, T), 1)
-        doc_of = first + (rc >> 4) * 4 + (rc & 3)
-        here = pick(doc_of == tc, starts, 1) - base == tc.astype(F32)
-        part = (rc >> 2) & 3
-        hots = [jnp.where(jnp.logical_and(here, part == c), 1.0, 0.0).astype(BF16) for c in range(4)]
-        halves = []
-        for h in range(2):
-            total = None
-            for c in range(4):
-                term = dot(hots[c], pool[:, c * C + h * 512 : c * C + (h + 1) * 512].astype(BF16))
-                total = term if total is None else total + term
-            halves.append(total.astype(BF16))
-        return halves
-
-    halves = gathered(SLOTS, z * 4)
-    for h in range(2):
-        s2[:, h * 512 : (h + 1) * 512] = halves[h]
-
-    def px_copy(w):
-        dst = rx.at[x, rows_of((w // NX) * 16, 16)]
-        return remote(s2.at[rows_of(w * 16, 16)], dst, px_snd.at[w], px_rcv.at[x, w // NX], (dp, z * NX + (z + w) % NX))
-
-    def px_wait(w, xx):
-        dst = rx.at[xx, rows_of((w // NX) * 16, 16)]
-        return remote(s2.at[rows_of(0, 16)], dst, px_snd.at[0], px_rcv.at[xx, w // NX], at_x(1))
-
-    def other_slots(fn):
-        @pl.loop(0, SLOTS)
-        def _(w):
-            @pl.when((z + w) % NX != x)
-            def _():
-                fn(w)
-
-    other_slots(lambda w: px_copy(w).start())
-
-    def pb_copy(c):
-        return remote(s2b.at[rows_of((c - HALF) * 16, 16)], rb, pb_snd.at[c - HALF], pb_rcv.at[0], (dp, c))
-
-    @pl.when(ctx == LAST)
-    def _():
-        halves = gathered(HALF, 4 * HALF)
-        for h in range(2):
-            s2b[:, h * 512 : (h + 1) * 512] = halves[h]
-
-        @pl.loop(HALF, LAST)
-        def _(c):
-            pb_copy(c).start()
-
-    q_sum, k_sum = lax.fori_loop(G // 2, G, scores, sums)
+    q_sum, k_sum = lax.fori_loop(0, G, scores, (zero, zero))
 
     def total_of(slots, count, copies):
         for copy in copies:
@@ -489,8 +502,6 @@
         def _():
             pz_copy(w).start()
 
-    each_slot(merge)
-
     @pl.loop(0, G // 2)
     def _(g):
         finish(g)
@@ -501,6 +512,8 @@
     @pl.loop(G // 2, G)
     def _(g):
         finish(g)
+
+    each_slot(merge)
 
     gx[spot] = total_of(gy, ny, y_pairs)
     send(x_pairs)
@@ -569,7 +582,7 @@
     row_copy(1).wait_send()
 
     def sent(w):
-        for i in range(1, NX):
+        for i in (1, NX - 1):
             cx_copy(w, i).wait_send()
 
         @pl.when(z + w != ctx)
@@ -577,6 +590,8 @@
             pz_copy(w).wait_send()
 
     each_slot(sent)
+    by_column(NX - 1, lambda w: cf_copy(w, 0).wait_send())
+    by_column(1, lambda w: cf_copy(w, 1).wait_send())
     other_slots(lambda w: px_copy(w).wait_send())
 
     @pl.when(keeps)
@@ -635,7 +650,6 @@
         vmem((G, R * T, 1), F32),
         vmem((G, R * T, 3 * T), F32),
         vmem((T, 3 * T), F32),
-        vmem((T, W), BF16),
         vmem((T, W), F32),
         vmem((T, W), F32),
         vmem((T, W), BF16),
@@ -667,6 +681,7 @@
         dma((2,)), dma((2,)),
         dma((NZ,)), dma((SLOTS,)),
         dma((SLOTS, NX)), dma((SLOTS,)),
+        dma((SLOTS,)), dma((SLOTS, 2)),
         dma((1,)), dma((HALF,)),
         dma((SLOTS,)), dma((NX, 3)),
         dma((3,)), dma((NZ,)),

time: 78.9 us -> 78.1 us (0.990)
  Pallas kernels: 78.1 us -> 77.2 us
    pallas_call x1, Pallas kernels: 75.8 us -> 74.9 us  [body(): pl.pallas_call(functools.partial(kernel, ny, nc), out_shape=(shape((4, C)...]
where the time goes in v4:
time: 78.1 us; the launch traced here: 77.9 us
  Pallas kernels  77.2 us (99%)
    pallas_call x1, Pallas kernels, body(): pl.pallas_call(functools.partial(kernel, ny, nc), out_shape=(shape((4, C)...  74.9 us
    pallas_call x1, Pallas kernels, body(): pl.pallas_call(emit, out_shape=tuple((shape(out.shape, out.dtype) for out...  2.32 us

profile of v4, /device:TPU:1, one launch (start us, length us, event | category | flops | bytes accessed | tf_op | source)
XLA Modules:
  0.0 77.9 jit_solution(5326490267842909334)
XLA Ops:
  0.6 74.9 %shard_map.134 = (f32[4,1024]{1,0:T(4,128)}, f32[4,2048]{1,0:T(4,128)}, f32[4,4096]{1,0:T(4,128)}, bf16[128,4096]{1,0:T(8,128)(2,1)}, bf16[128,1024]{1,0:T(8,128...) custom-call(bf16[128,4096]{1,0:T(8,128)(2,1)} %bitcast.14, bf16[128,1024]{1,0:T(8,128)(2,1)} %bitcast.15, ...), custom_call_target="tpu_custom_call" | custom-call | tf_op jit(solution)/shard_map/pallas_call | solution.py:695
  75.5 2.3 %shard_map.135 = (f32[4,1024]{1,0:T(4,128)}, f32[4,2048]{1,0:T(4,128)}, f32[4,4096]{1,0:T(4,128)}, bf16[128,4096]{1,0:T(8,128)(2,1)}, bf16[128,1024]{1,0:T(8,128...) custom-call(f32[4,1024]{1,0:T(4,128)} %get-tuple-element.24.refs_0_, ...), custom_call_target="tpu_custom_call" | custom-call | tf_op jit(solution)/shard_map/pallas_call | solution.py:717

commit v5 on v4

--- a/solution.py
+++ b/solution.py
@@ -502,16 +502,12 @@
         def _():
             pz_copy(w).start()
 
-    @pl.loop(0, G // 2)
+    @pl.loop(0, G)
     def _(g):
         finish(g)
 
     gy[y] = total_of(gz, NZ, z_pairs)
     send(y_pairs)
-
-    @pl.loop(G // 2, G)
-    def _(g):
-        finish(g)
 
     each_slot(merge)
 

time: 78.1 us -> 78.9 us (1.010)
  Pallas kernels: 77.2 us -> 78 us
    pallas_call x1, Pallas kernels: 74.9 us -> 75.7 us  [body(): pl.pallas_call(functools.partial(kernel, ny, nc), out_shape=(shape((4, C)...]
where the time goes in v5:
time: 78.9 us; the launch traced here: 78.7 us
  Pallas kernels  78 us (99%)
    pallas_call x1, Pallas kernels, body(): pl.pallas_call(functools.partial(kernel, ny, nc), out_shape=(shape((4, C)...  75.7 us
    pallas_call x1, Pallas kernels, body(): pl.pallas_call(emit, out_shape=tuple((shape(out.shape, out.dtype) for out...  2.32 us

profile of v5, /device:TPU:1, one launch (start us, length us, event | category | flops | bytes accessed | tf_op | source)
XLA Modules:
  0.0 78.7 jit_solution(914301509093976286)
XLA Ops:
  0.6 75.7 %shard_map.134 = (f32[4,1024]{1,0:T(4,128)}, f32[4,2048]{1,0:T(4,128)}, f32[4,4096]{1,0:T(4,128)}, bf16[128,4096]{1,0:T(8,128)(2,1)}, bf16[128,1024]{1,0:T(8,128...) custom-call(bf16[128,4096]{1,0:T(8,128)(2,1)} %bitcast.14, bf16[128,1024]{1,0:T(8,128)(2,1)} %bitcast.15, ...), custom_call_target="tpu_custom_call" | custom-call | tf_op jit(solution)/shard_map/pallas_call | solution.py:691
  76.4 2.3 %shard_map.135 = (f32[4,1024]{1,0:T(4,128)}, f32[4,2048]{1,0:T(4,128)}, f32[4,4096]{1,0:T(4,128)}, bf16[128,4096]{1,0:T(8,128)(2,1)}, bf16[128,1024]{1,0:T(8,128...) custom-call(f32[4,1024]{1,0:T(4,128)} %get-tuple-element.24.refs_0_, ...), custom_call_target="tpu_custom_call" | custom-call | tf_op jit(solution)/shard_map/pallas_call | solution.py:713
